TPU v7x, 32 devices: a whole 2x2x4 slice. The times are simulated.
32 devices in a mesh: tile: 8 (over z, y), cplx: 4 (over x, core).
Axes of the slice: x: 2, y: 2, z: 4, core: 2. Of those that a mesh axis runs over, the one named last changes fastest.
Arguments:
- pair_tiles: bfloat16 [96, 128, 128, 128], P(('tile', 'cplx'))
- tile_map: int32 [96, 3], replicated, may hold values from -1 to 3, as said below
- lengths: int32 [4], replicated, may hold values from 256 to 512
- resolved: int32 [4, 512], replicated, may hold values 0 or 1
- ln_gain: float32 [128], replicated, may hold values from 0.1 to 1.9
- w_in: bfloat16 [128, 512], replicated, may hold values from -0.5 to 0.5
- w_out: bfloat16 [512, 128], replicated, may hold values from -0.25 to 0.25
- w_head: bfloat16 [128, 64], replicated
- head_bias: float32 [64], replicated, may hold values from -4 to 4
Outputs:
- error_map: float32 [4, 512, 512], P('cplx', 'tile')
- residue_error: float32 [4, 512], P('cplx', 'tile')
- tm_score: float32 [4], P('cplx')
Inputs may be any that keep to these rules, and one draw needn't show every extreme that they name: `tile_map`: row (t * 4 + c) * 3 + j is slot j of the device at tile index t and cplx index c and holds the complex, block row and block column of its tile, or -1 three times where the slot is empty. Each tile (k, r, q) with r and q below ceil(lengths[k] / 128) is held by exactly one slot and no other tile is held. Complex k is owned by cplx index k // 1; no two filled slots of one device have the same owner, and for fixed t and j the owners over the 4 cplx indices are all different.
All inputs are finite; a program needn't handle non-finite values.
Results may differ from a plain program's by a relative error of at most 0.0089.
Values sent between devices are 32-bit elements; how exact they have to be, the bound alone decides.
No kernel may reach another device: no remote copies, remote signals or barrier semaphores. Data moves between devices by JAX's collectives and lax.ppermute only.
A program may use at most 128 MiB of HBM per device.

v0:
```python
import jax
import jax.numpy as jnp
from jax import lax
from jax.sharding import PartitionSpec as P

EPS = 1e-05


def bin_centers(bin_count):
    bin_step = 31.0 / (bin_count - 2)
    return (jnp.arange(bin_count, dtype=jnp.float32) + 0.5) * bin_step


def d_zero(length):
    clipped = jnp.maximum(length, 19).astype(jnp.float32)
    return 1.24 * jnp.cbrt(clipped - 15.0) - 1.8


def pair_head(row_block, ln_gain, w_in, w_out, w_head, head_bias, centers, distance):
    values = row_block.astype(jnp.float32)
    row_mean = jnp.mean(values, axis=-1, keepdims=True)
    centred = values - row_mean
    variance = jnp.mean(centred * centred, axis=-1, keepdims=True)
    normed = (centred * lax.rsqrt(variance + EPS) * ln_gain).astype(jnp.bfloat16)
    hidden = jax.nn.relu(jnp.dot(normed, w_in, preferred_element_type=jnp.float32)).astype(
        jnp.bfloat16
    )
    updated = (values + jnp.dot(hidden, w_out, preferred_element_type=jnp.float32)).astype(
        jnp.bfloat16
    )
    logits = jnp.dot(updated, w_head, preferred_element_type=jnp.float32) + head_bias
    bin_probs = jax.nn.softmax(logits, axis=-1)
    expected = jnp.sum(bin_probs * centers, axis=-1)
    tm_term = jnp.sum(bin_probs / (1.0 + (centers / distance) ** 2), axis=-1)
    return (expected, tm_term)


def route_rows(
    error_src, rows_src, row_src, found_src, n_tile, parts_per, rows_each, tile_side, highest
):
    target_rows = jnp.arange(n_tile, dtype=jnp.int32)[:, None, None]
    part_index = jnp.arange(parts_per, dtype=jnp.int32)[None, None, :]
    routing = (
        (target_rows == row_src[None, :, None] * parts_per + part_index) & found_src[None, :, None]
    ).astype(jnp.float32)
    sender_count = error_src.shape[0]
    error_parts = error_src.reshape(sender_count, parts_per, rows_each, tile_side)
    row_parts = rows_src.reshape(sender_count, parts_per, rows_each)
    error_out = jnp.einsum("tcq,cqrj->tcrj", routing, error_parts, precision=highest)
    rows_out = jnp.einsum("tcq,cqr->tcr", routing, row_parts, precision=highest)
    return (error_out, rows_out)


def place_rows(
    error_back,
    rows_back,
    member_all,
    row_all,
    colblk_all,
    found_all,
    row_index,
    parts_per,
    cpx_dev,
    blocks,
    rows_each,
    tile_side,
    maxres,
    highest,
):
    mine_rows = found_all & (row_all == row_index // parts_per)
    member_hot = (
        (jnp.arange(cpx_dev, dtype=jnp.int32)[None, None, :] == member_all[..., None])
        & mine_rows[..., None]
    ).astype(jnp.float32)
    block_hot = (
        jnp.arange(blocks, dtype=jnp.int32)[None, None, :] == colblk_all[..., None]
    ).astype(jnp.float32)
    sources = member_all.shape[0] * member_all.shape[1]
    place_hot = (member_hot[..., :, None] * block_hot[..., None, :]).reshape(
        sources, cpx_dev, blocks
    )
    share_map = jnp.einsum(
        "smb,srj->mrbj",
        place_hot,
        error_back.reshape(sources, rows_each, tile_side),
        precision=highest,
    ).reshape(cpx_dev, rows_each, maxres)
    share_rows = jnp.einsum(
        "sm,sr->mr",
        member_hot.reshape(sources, cpx_dev),
        rows_back.reshape(sources, rows_each),
        precision=highest,
    )
    return (share_map, share_rows)


def shards(pair_tiles, tile_map, lengths, resolved, ln_gain, w_in, w_out, w_head, head_bias):
    highest = lax.Precision.HIGHEST
    n_tile = lax.axis_size("tile")
    n_cplx = lax.axis_size("cplx")
    row_index = lax.axis_index("tile")
    col_index = lax.axis_index("cplx")
    slot_count, tile_side, _, pair_width = pair_tiles.shape
    complexes, maxres = resolved.shape
    blocks = maxres // tile_side
    cpx_dev = complexes // n_cplx
    rows_each = maxres // n_tile
    parts_per = tile_side // rows_each
    centers = bin_centers(w_head.shape[1])
    positions = jnp.arange(maxres, dtype=jnp.int32)
    valid_mask = ((positions[None, :] < lengths[:, None]) & (resolved > 0)).astype(jnp.float32)
    valid_blocks = valid_mask.reshape(complexes, blocks, tile_side)
    layout = tile_map.reshape(n_tile, n_cplx, slot_count, 3)
    own_slots = layout[row_index, col_index]
    row_count = tile_side * tile_side
    block_rows = min(4096, row_count)
    error_tiles = []
    score_tiles = []
    owner_list = []
    for slot in range(slot_count):
        slot_meta = own_slots[slot]
        present = slot_meta[0] >= 0
        complex_id = jnp.maximum(slot_meta[0], 0)
        block_row = jnp.maximum(slot_meta[1], 0)
        block_col = jnp.maximum(slot_meta[2], 0)
        distance = d_zero(lengths[complex_id])

        def head_block(row_block, distance=distance):
            return pair_head(row_block, ln_gain, w_in, w_out, w_head, head_bias, centers, distance)

        expected, tm_term = lax.map(
            head_block, pair_tiles[slot].reshape(row_count // block_rows, block_rows, pair_width)
        )
        row_valid = valid_blocks[complex_id, block_row]
        col_valid = valid_blocks[complex_id, block_col]
        weight = jnp.where(present, row_valid[:, None] * col_valid[None, :], jnp.float32(0.0))
        error_tiles.append(weight * expected.reshape(tile_side, tile_side))
        score_tiles.append(weight * tm_term.reshape(tile_side, tile_side))
        owner_list.append(jnp.where(present, complex_id // cpx_dev, -1))
    owner_ids = jnp.stack(owner_list)
    select = (jnp.arange(n_cplx, dtype=jnp.int32)[:, None] == owner_ids[None, :]).astype(
        jnp.float32
    )
    error_send = jnp.einsum("os,sij->oij", select, jnp.stack(error_tiles), precision=highest)
    score_send = jnp.einsum("os,sij->oij", select, jnp.stack(score_tiles), precision=highest)
    error_in, score_in = (
        lax.all_to_all(error_send, "cplx", split_axis=0, concat_axis=0, tiled=True),
        lax.all_to_all(score_send, "cplx", split_axis=0, concat_axis=0, tiled=True),
    )
    rows_in = jnp.sum(score_in, axis=2)
    complex_all = layout[..., 0]
    owner_all = jnp.where(complex_all >= 0, complex_all // cpx_dev, -1)
    matched = owner_all == col_index
    matched_float = matched.astype(jnp.float32)
    slot_hot = matched_float[row_index]
    error_slots = jnp.einsum("sj,sab->jab", slot_hot, error_in, precision=highest)
    rows_slots = jnp.einsum("sj,sa->ja", slot_hot, rows_in, precision=highest)
    found_slot = jnp.any(matched, axis=1)

    def pick_slot(column):
        return jnp.sum(jnp.where(matched, layout[..., column], 0), axis=1)

    member_slot = pick_slot(0) - col_index * cpx_dev
    row_slot = pick_slot(1)
    colblk_slot = pick_slot(2)
    error_out, rows_out = route_rows(
        error_slots,
        rows_slots,
        row_slot[row_index],
        found_slot[row_index],
        n_tile,
        parts_per,
        rows_each,
        tile_side,
        highest,
    )
    error_back, rows_back = (
        lax.all_to_all(error_out, "tile", split_axis=0, concat_axis=0, tiled=True),
        lax.all_to_all(rows_out, "tile", split_axis=0, concat_axis=0, tiled=True),
    )
    share_map, share_rows = place_rows(
        error_back,
        rows_back,
        member_slot,
        row_slot,
        colblk_slot,
        found_slot,
        row_index,
        parts_per,
        cpx_dev,
        blocks,
        rows_each,
        tile_side,
        maxres,
        highest,
    )
    valid_rows = lax.dynamic_slice(
        valid_mask, (col_index * cpx_dev, row_index * rows_each), (cpx_dev, rows_each)
    )
    totals = lax.dynamic_slice_in_dim(jnp.sum(valid_mask, axis=1), col_index * cpx_dev, cpx_dev)
    denominator = jnp.maximum(valid_rows * totals[:, None], jnp.float32(1.0))
    residue_error = jnp.sum(share_map, axis=2) / denominator
    best_share = jnp.max(share_rows / denominator, axis=1)
    tm_score = lax.pmax(best_share, "tile")
    return (share_map, residue_error, tm_score)


def solution(mesh):
    placed = (P(("tile", "cplx"), None, None, None), P(), P(), P(), P(), P(), P(), P(), P())
    return jax.shard_map(
        shards,
        mesh=mesh,
        in_specs=placed,
        out_specs=(P("cplx", "tile", None), P("cplx", "tile"), P("cplx")),
        check_vma=False,
    )
```

profile of v0, /device:TPU:0, one launch (start us, length us, event | category | flops | bytes accessed | tf_op | source)
XLA Modules:
  0.0 221.4 jit_solution(597201668748234575)
XLA Ops:
  6.2 8.9 %fusion.147 = (bf16[1,128,128,128]{3,2,1,0:T(8,128)(2,1)}, bf16[1,128,128,128]{3,2,1,0:T(8,128)(2,1)}, bf16[1,128,128,128]{3,2,1,0:T(8,128)(2,1)}) fusion(bf16[3,128,128,128]{3,2,1,0:T(8,128)(2,1)} %param.15), kind=kLoop, calls=%fused_computation.187 | loop fusion | bytes 25165824 | tf_op jit(solution)/shard_map/slice | solution.py:132
  16.5 38.7 %while.44 = (s32[]{:T(128)}, f32[4,4096]{1,0:T(4,128)S(1)}, f32[4,4096]{1,0:T(4,128)S(1)}, bf16[4,4096,128]{2,1,0:T(8,128)(2,1)}, f32[128]{0:T(128)S(1)}, /*inde...) while((s32[]{:T(128)}, f32[4,4096]{1,0:T(4,128)S(1)}, ...), condition=%wide.region_23.24_spmd.clone.clone, body=%wide.region_16.23_spmd.clone.clone.sunk | while | flops 1155256576 | bytes 10046353 | solution.py:131
  18.1 2.3 %fusion.225 = f32[4096]{0:T(1024)S(1)} fusion(f32[4096]{0:T(1024)S(1)} %broadcast_multiply_fusion.8, bf16[4,4096,128]{2,1,0:T(8,128)(2,1)} %get-tuple-element.704, s32[]{:T(128)S(6)} %copy.88), kind=kLoop, calls=%fused_computation.68.clone.1 | loop fusion | flops 2093056 | bytes 1081348 | tf_op jit(solution)/shard_map/while/body/eval_jaxpr/reduce_sum | solution.py:23
  20.4 4.1 %fusion.226 = bf16[4096,128]{1,0:T(8,128)(2,1)S(1)} fusion(bf16[512,128]{1,0:T(8,128)(2,1)S(1)} %get-tuple-element.707, bf16[128,512]{1,0:T(8,128)(2,1)S(1)} %get-tuple-element.706, f32[128]{0:T(128)S(1)} %get-tuple-element.705, f32[4096]{0:T(1024)S(1)} %add_rsqrt_fusion.8, f32[4096]{0:T(1024)S(1)} %broadcast_multiply_fusion.8, ...), kind=kOutput, calls=%fused_computation.61.clone.1 | convolution fusion | flops 1082130432 | bytes 3442176 | tf_op jit(solution)/shard_map/while/body/eval_jaxpr/dot_general | solution.py:28
  27.8 2.3 %fusion.225 = f32[4096]{0:T(1024)S(1)} fusion(f32[4096]{0:T(1024)S(1)} %broadcast_multiply_fusion.8, bf16[4,4096,128]{2,1,0:T(8,128)(2,1)} %get-tuple-element.704, s32[]{:T(128)S(6)} %copy.88), kind=kLoop, calls=%fused_computation.68.clone.1 | loop fusion | flops 2093056 | bytes 1081348 | tf_op jit(solution)/shard_map/while/body/eval_jaxpr/reduce_sum | solution.py:23
  30.2 4.0 %fusion.226 = bf16[4096,128]{1,0:T(8,128)(2,1)S(1)} fusion(bf16[512,128]{1,0:T(8,128)(2,1)S(1)} %get-tuple-element.707, bf16[128,512]{1,0:T(8,128)(2,1)S(1)} %get-tuple-element.706, f32[128]{0:T(128)S(1)} %get-tuple-element.705, f32[4096]{0:T(1024)S(1)} %add_rsqrt_fusion.8, f32[4096]{0:T(1024)S(1)} %broadcast_multiply_fusion.8, ...), kind=kOutput, calls=%fused_computation.61.clone.1 | convolution fusion | flops 1082130432 | bytes 3442176 | tf_op jit(solution)/shard_map/while/body/eval_jaxpr/dot_general | solution.py:28
  37.5 2.3 %fusion.225 = f32[4096]{0:T(1024)S(1)} fusion(f32[4096]{0:T(1024)S(1)} %broadcast_multiply_fusion.8, bf16[4,4096,128]{2,1,0:T(8,128)(2,1)} %get-tuple-element.704, s32[]{:T(128)S(6)} %copy.88), kind=kLoop, calls=%fused_computation.68.clone.1 | loop fusion | flops 2093056 | bytes 1081348 | tf_op jit(solution)/shard_map/while/body/eval_jaxpr/reduce_sum | solution.py:23
  39.8 4.2 %fusion.226 = bf16[4096,128]{1,0:T(8,128)(2,1)S(1)} fusion(bf16[512,128]{1,0:T(8,128)(2,1)S(1)} %get-tuple-element.707, bf16[128,512]{1,0:T(8,128)(2,1)S(1)} %get-tuple-element.706, f32[128]{0:T(128)S(1)} %get-tuple-element.705, f32[4096]{0:T(1024)S(1)} %add_rsqrt_fusion.8, f32[4096]{0:T(1024)S(1)} %broadcast_multiply_fusion.8, ...), kind=kOutput, calls=%fused_computation.61.clone.1 | convolution fusion | flops 1082130432 | bytes 3442176 | tf_op jit(solution)/shard_map/while/body/eval_jaxpr/dot_general | solution.py:28
  47.2 2.3 %fusion.225 = f32[4096]{0:T(1024)S(1)} fusion(f32[4096]{0:T(1024)S(1)} %broadcast_multiply_fusion.8, bf16[4,4096,128]{2,1,0:T(8,128)(2,1)} %get-tuple-element.704, s32[]{:T(128)S(6)} %copy.88), kind=kLoop, calls=%fused_computation.68.clone.1 | loop fusion | flops 2093056 | bytes 1081348 | tf_op jit(solution)/shard_map/while/body/eval_jaxpr/reduce_sum | solution.py:23
  49.6 4.0 %fusion.226 = bf16[4096,128]{1,0:T(8,128)(2,1)S(1)} fusion(bf16[512,128]{1,0:T(8,128)(2,1)S(1)} %get-tuple-element.707, bf16[128,512]{1,0:T(8,128)(2,1)S(1)} %get-tuple-element.706, f32[128]{0:T(128)S(1)} %get-tuple-element.705, f32[4096]{0:T(1024)S(1)} %add_rsqrt_fusion.8, f32[4096]{0:T(1024)S(1)} %broadcast_multiply_fusion.8, ...), kind=kOutput, calls=%fused_computation.61.clone.1 | convolution fusion | flops 1082130432 | bytes 3442176 | tf_op jit(solution)/shard_map/while/body/eval_jaxpr/dot_general | solution.py:28
  60.1 39.0 %while.42 = (s32[]{:T(128)}, f32[4,4096]{1,0:T(4,128)S(1)}, f32[4,4096]{1,0:T(4,128)S(1)}, bf16[4,4096,128]{2,1,0:T(8,128)(2,1)}, f32[128]{0:T(128)S(1)}, /*inde...) while((s32[]{:T(128)}, f32[4,4096]{1,0:T(4,128)S(1)}, ...), condition=%wide.region_7.8_spmd.clone.clone, body=%wide.region_0.7_spmd.clone.clone.sunk | while | flops 1155256576 | bytes 10046353 | solution.py:131
  61.7 2.3 %fusion.203 = f32[4096]{0:T(1024)S(1)} fusion(f32[4096]{0:T(1024)S(1)} %broadcast_multiply_fusion.6, bf16[4,4096,128]{2,1,0:T(8,128)(2,1)} %get-tuple-element.740, s32[]{:T(128)S(6)} %copy.97), kind=kLoop, calls=%fused_computation.12.clone.1 | loop fusion | flops 2093056 | bytes 1081348 | tf_op jit(solution)/shard_map/while/body/eval_jaxpr/reduce_sum | solution.py:23
  64.0 4.1 %fusion.204 = bf16[4096,128]{1,0:T(8,128)(2,1)S(1)} fusion(bf16[512,128]{1,0:T(8,128)(2,1)S(1)} %get-tuple-element.743, bf16[128,512]{1,0:T(8,128)(2,1)S(1)} %get-tuple-element.742, f32[128]{0:T(128)S(1)} %get-tuple-element.741, f32[4096]{0:T(1024)S(1)} %add_rsqrt_fusion.6, f32[4096]{0:T(1024)S(1)} %broadcast_multiply_fusion.6, ...), kind=kOutput, calls=%fused_computation.5.clone.1 | convolution fusion | flops 1082130432 | bytes 3442176 | tf_op jit(solution)/shard_map/while/body/eval_jaxpr/dot_general | solution.py:28
  71.4 2.3 %fusion.203 = f32[4096]{0:T(1024)S(1)} fusion(f32[4096]{0:T(1024)S(1)} %broadcast_multiply_fusion.6, bf16[4,4096,128]{2,1,0:T(8,128)(2,1)} %get-tuple-element.740, s32[]{:T(128)S(6)} %copy.97), kind=kLoop, calls=%fused_computation.12.clone.1 | loop fusion | flops 2093056 | bytes 1081348 | tf_op jit(solution)/shard_map/while/body/eval_jaxpr/reduce_sum | solution.py:23
  73.7 4.1 %fusion.204 = bf16[4096,128]{1,0:T(8,128)(2,1)S(1)} fusion(bf16[512,128]{1,0:T(8,128)(2,1)S(1)} %get-tuple-element.743, bf16[128,512]{1,0:T(8,128)(2,1)S(1)} %get-tuple-element.742, f32[128]{0:T(128)S(1)} %get-tuple-element.741, f32[4096]{0:T(1024)S(1)} %add_rsqrt_fusion.6, f32[4096]{0:T(1024)S(1)} %broadcast_multiply_fusion.6, ...), kind=kOutput, calls=%fused_computation.5.clone.1 | convolution fusion | flops 1082130432 | bytes 3442176 | tf_op jit(solution)/shard_map/while/body/eval_jaxpr/dot_general | solution.py:28
  81.1 2.3 %fusion.203 = f32[4096]{0:T(1024)S(1)} fusion(f32[4096]{0:T(1024)S(1)} %broadcast_multiply_fusion.6, bf16[4,4096,128]{2,1,0:T(8,128)(2,1)} %get-tuple-element.740, s32[]{:T(128)S(6)} %copy.97), kind=kLoop, calls=%fused_computation.12.clone.1 | loop fusion | flops 2093056 | bytes 1081348 | tf_op jit(solution)/shard_map/while/body/eval_jaxpr/reduce_sum | solution.py:23
  83.4 4.2 %fusion.204 = bf16[4096,128]{1,0:T(8,128)(2,1)S(1)} fusion(bf16[512,128]{1,0:T(8,128)(2,1)S(1)} %get-tuple-element.743, bf16[128,512]{1,0:T(8,128)(2,1)S(1)} %get-tuple-element.742, f32[128]{0:T(128)S(1)} %get-tuple-element.741, f32[4096]{0:T(1024)S(1)} %add_rsqrt_fusion.6, f32[4096]{0:T(1024)S(1)} %broadcast_multiply_fusion.6, ...), kind=kOutput, calls=%fused_computation.5.clone.1 | convolution fusion | flops 1082130432 | bytes 3442176 | tf_op jit(solution)/shard_map/while/body/eval_jaxpr/dot_general | solution.py:28
  93.2 4.2 %fusion.204 = bf16[4096,128]{1,0:T(8,128)(2,1)S(1)} fusion(bf16[512,128]{1,0:T(8,128)(2,1)S(1)} %get-tuple-element.743, bf16[128,512]{1,0:T(8,128)(2,1)S(1)} %get-tuple-element.742, f32[128]{0:T(128)S(1)} %get-tuple-element.741, f32[4096]{0:T(1024)S(1)} %add_rsqrt_fusion.6, f32[4096]{0:T(1024)S(1)} %broadcast_multiply_fusion.6, ...), kind=kOutput, calls=%fused_computation.5.clone.1 | convolution fusion | flops 1082130432 | bytes 3442176 | tf_op jit(solution)/shard_map/while/body/eval_jaxpr/dot_general | solution.py:28
  100.0 38.7 %while.43 = (s32[]{:T(128)}, f32[4,4096]{1,0:T(4,128)S(1)}, f32[4,4096]{1,0:T(4,128)S(1)}, bf16[4,4096,128]{2,1,0:T(8,128)(2,1)}, f32[128]{0:T(128)S(1)}, /*inde...) while((s32[]{:T(128)}, f32[4,4096]{1,0:T(4,128)S(1)}, ...), condition=%wide.region_15.16_spmd.clone.clone, body=%wide.region_8.15_spmd.clone.clone.sunk | while | flops 1155256576 | bytes 10046353 | solution.py:131
  103.9 4.0 %fusion.215 = bf16[4096,128]{1,0:T(8,128)(2,1)S(1)} fusion(bf16[512,128]{1,0:T(8,128)(2,1)S(1)} %get-tuple-element.779, bf16[128,512]{1,0:T(8,128)(2,1)S(1)} %get-tuple-element.778, f32[128]{0:T(128)S(1)} %get-tuple-element.777, f32[4096]{0:T(1024)S(1)} %add_rsqrt_fusion.7, f32[4096]{0:T(1024)S(1)} %broadcast_multiply_fusion.7, ...), kind=kOutput, calls=%fused_computation.33.clone.1 | convolution fusion | flops 1082130432 | bytes 3442176 | tf_op jit(solution)/shard_map/while/body/eval_jaxpr/dot_general | solution.py:28
  113.5 4.0 %fusion.215 = bf16[4096,128]{1,0:T(8,128)(2,1)S(1)} fusion(bf16[512,128]{1,0:T(8,128)(2,1)S(1)} %get-tuple-element.779, bf16[128,512]{1,0:T(8,128)(2,1)S(1)} %get-tuple-element.778, f32[128]{0:T(128)S(1)} %get-tuple-element.777, f32[4096]{0:T(1024)S(1)} %add_rsqrt_fusion.7, f32[4096]{0:T(1024)S(1)} %broadcast_multiply_fusion.7, ...), kind=kOutput, calls=%fused_computation.33.clone.1 | convolution fusion | flops 1082130432 | bytes 3442176 | tf_op jit(solution)/shard_map/while/body/eval_jaxpr/dot_general | solution.py:28
  123.2 4.0 %fusion.215 = bf16[4096,128]{1,0:T(8,128)(2,1)S(1)} fusion(bf16[512,128]{1,0:T(8,128)(2,1)S(1)} %get-tuple-element.779, bf16[128,512]{1,0:T(8,128)(2,1)S(1)} %get-tuple-element.778, f32[128]{0:T(128)S(1)} %get-tuple-element.777, f32[4096]{0:T(1024)S(1)} %add_rsqrt_fusion.7, f32[4096]{0:T(1024)S(1)} %broadcast_multiply_fusion.7, ...), kind=kOutput, calls=%fused_computation.33.clone.1 | convolution fusion | flops 1082130432 | bytes 3442176 | tf_op jit(solution)/shard_map/while/body/eval_jaxpr/dot_general | solution.py:28
  132.7 4.1 %fusion.215 = bf16[4096,128]{1,0:T(8,128)(2,1)S(1)} fusion(bf16[512,128]{1,0:T(8,128)(2,1)S(1)} %get-tuple-element.779, bf16[128,512]{1,0:T(8,128)(2,1)S(1)} %get-tuple-element.778, f32[128]{0:T(128)S(1)} %get-tuple-element.777, f32[4096]{0:T(1024)S(1)} %add_rsqrt_fusion.7, f32[4096]{0:T(1024)S(1)} %broadcast_multiply_fusion.7, ...), kind=kOutput, calls=%fused_computation.33.clone.1 | convolution fusion | flops 1082130432 | bytes 3442176 | tf_op jit(solution)/shard_map/while/body/eval_jaxpr/dot_general | solution.py:28
  140.8 4.2 %all-to-all-start = ((f32[4,128,128]{2,1,0:T(8,128)}), f32[4,128,128]{2,1,0:T(8,128)S(1)}, u32[]{:S(2)}, u32[]{:S(2)}) async-start(f32[4,128,128]{2,1,0:T(8,128)} %copy.42), calls=%async_computation | async-start | bytes 524288 | tf_op jit(solution)/shard_map/all_to_all | solution.py:147
  147.4 3.6 %all-to-all-done = f32[4,128,128]{2,1,0:T(8,128)S(1)} async-done(((f32[4,128,128]{2,1,0:T(8,128)}), f32[4,128,128]{2,1,0:T(8,128)S(1)}, u32[]{:S(2)}, u32[]{:S(2)}) %all-to-all-start) | async-done | bytes 262176 | tf_op jit(solution)/shard_map/all_to_all | solution.py:147
  151.1 3.4 %all-to-all-start.2 = ((f32[4,128,128]{2,1,0:T(8,128)}), f32[4,128,128]{2,1,0:T(8,128)S(1)}, u32[]{:S(2)}, u32[]{:S(2)}) async-start(f32[4,128,128]{2,1,0:T(8,128)} %copy.52), calls=%async_computation.2 | async-start | bytes 524288 | tf_op jit(solution)/shard_map/all_to_all | solution.py:148
  155.0 5.4 %all-to-all-done.2 = f32[4,128,128]{2,1,0:T(8,128)S(1)} async-done(((f32[4,128,128]{2,1,0:T(8,128)}), f32[4,128,128]{2,1,0:T(8,128)S(1)}, u32[]{:S(2)}, u32[]{:S(2)}) %all-to-all-start.2) | async-done | bytes 262176 | tf_op jit(solution)/shard_map/all_to_all | solution.py:148
  161.9 6.4 %all-to-all-start.3 = ((f32[8,1,192]{2,1,0:T(1,128)}), f32[8,1,192]{2,1,0:T(1,128)S(1)}, u32[]{:S(2)}, u32[]{:S(2)}) async-start(f32[8,1,192]{2,1,0:T(1,128)} %reshape.699), calls=%async_computation.3 | async-start | bytes 16384 | tf_op jit(solution)/shard_map/all_to_all | solution.py:179
  170.0 4.9 %all-to-all-done.3 = f32[8,1,192]{2,1,0:T(1,128)S(1)} async-done(((f32[8,1,192]{2,1,0:T(1,128)}), f32[8,1,192]{2,1,0:T(1,128)S(1)}, u32[]{:S(2)}, u32[]{:S(2)}) %all-to-all-start.3) | async-done | bytes 6176 | tf_op jit(solution)/shard_map/all_to_all | solution.py:179
  174.9 3.5 %all-to-all-start.1 = ((f32[8,3,64,128]{3,2,1,0:T(8,128)}), f32[8,3,64,128]{3,2,1,0:T(8,128)S(1)}, u32[]{:S(2)}, u32[]{:S(2)}) async-start(f32[8,3,64,128]{3,2,1,0:T(8,128)} %copy.47), calls=%async_computation.1 | async-start | bytes 1572864 | tf_op jit(solution)/shard_map/all_to_all | solution.py:178
  180.6 16.5 %all-to-all-done.1 = f32[8,3,64,128]{3,2,1,0:T(8,128)S(1)} async-done(((f32[8,3,64,128]{3,2,1,0:T(8,128)}), f32[8,3,64,128]{3,2,1,0:T(8,128)S(1)}, u32[]{:S(2)}, u32[]{:S(2)}) %all-to-all-start.1) | async-done | bytes 786464 | tf_op jit(solution)/shard_map/all_to_all | solution.py:178
  201.4 20.0 %pmax.7 = f32[1]{0:T(128)} all-reduce(f32[1]{0:T(128)} %bitcast.53), channel_id=1, replica_groups=mesh['tile'=8,'cplx'=4] {'tile'}, use_global_device_ids=true, to_apply=%region_32.33 | all-reduce | flops 1 | bytes 8 | tf_op jit(solution)/shard_map/pmax | solution.py:204
  (187 shorter events, 67.2 us)
Async XLA Ops:
  6.1 9.0 %copy-start.3 = (s32[4]{0:T(128)S(1)}, s32[4]{0:T(128)}, u32[]{:S(2)}) copy-start(s32[4]{0:T(128)} %param.17) | copy-start | bytes 52
  6.1 10.3 %copy-start = (bf16[128,64]{0,1:T(8,128)(2,1)S(1)}, bf16[128,64]{0,1:T(8,128)(2,1)}, u32[]{:S(2)}) copy-start(bf16[128,64]{0,1:T(8,128)(2,1)} %param.22) | copy-start | bytes 49156
  6.2 10.3 %copy-start.1 = (f32[64]{0:T(128)S(1)}, f32[64]{0:T(128)}, u32[]{:S(2)}) copy-start(f32[64]{0:T(128)} %param.23) | copy-start | bytes 772
  6.2 10.3 %copy-start.4 = (bf16[128,512]{1,0:T(8,128)(2,1)S(1)}, bf16[128,512]{1,0:T(8,128)(2,1)}, u32[]{:S(2)}) copy-start(bf16[128,512]{1,0:T(8,128)(2,1)} %param.20) | copy-start | bytes 393220
  6.2 10.3 %copy-start.5 = (bf16[512,128]{1,0:T(8,128)(2,1)S(1)}, bf16[512,128]{1,0:T(8,128)(2,1)}, u32[]{:S(2)}) copy-start(bf16[512,128]{1,0:T(8,128)(2,1)} %param.21) | copy-start | bytes 393220
  6.2 10.3 %copy-start.6 = (f32[128]{0:T(128)S(1)}, f32[128]{0:T(128)}, u32[]{:S(2)}) copy-start(f32[128]{0:T(128)} %param.19) | copy-start | bytes 1540
  16.5 38.8 %copy-start.2 = (s32[4,512]{1,0:T(4,128)S(1)}, s32[4,512]{1,0:T(4,128)}, u32[]{:S(2)}) copy-start(s32[4,512]{1,0:T(4,128)} %param.18) | copy-start | bytes 24580
  140.8 10.2 %all-to-all-start = ((f32[4,128,128]{2,1,0:T(8,128)}), f32[4,128,128]{2,1,0:T(8,128)S(1)}, u32[]{:S(2)}, u32[]{:S(2)}) async-start(f32[4,128,128]{2,1,0:T(8,128)} %copy.42), calls=%async_computation | async-start | bytes 524288 | tf_op jit(solution)/shard_map/all_to_all | solution.py:147
  151.1 9.4 %all-to-all-start.2 = ((f32[4,128,128]{2,1,0:T(8,128)}), f32[4,128,128]{2,1,0:T(8,128)S(1)}, u32[]{:S(2)}, u32[]{:S(2)}) async-start(f32[4,128,128]{2,1,0:T(8,128)} %copy.52), calls=%async_computation.2 | async-start | bytes 524288 | tf_op jit(solution)/shard_map/all_to_all | solution.py:148
  161.9 13.0 %all-to-all-start.3 = ((f32[8,1,192]{2,1,0:T(1,128)}), f32[8,1,192]{2,1,0:T(1,128)S(1)}, u32[]{:S(2)}, u32[]{:S(2)}) async-start(f32[8,1,192]{2,1,0:T(1,128)} %reshape.699), calls=%async_computation.3 | async-start | bytes 16384 | tf_op jit(solution)/shard_map/all_to_all | solution.py:179
  174.9 22.3 %all-to-all-start.1 = ((f32[8,3,64,128]{3,2,1,0:T(8,128)}), f32[8,3,64,128]{3,2,1,0:T(8,128)S(1)}, u32[]{:S(2)}, u32[]{:S(2)}) async-start(f32[8,3,64,128]{3,2,1,0:T(8,128)} %copy.47), calls=%async_computation.1 | async-start | bytes 1572864 | tf_op jit(solution)/shard_map/all_to_all | solution.py:178
where the time goes:
time: 223 us; the launch traced here: 221 us
  matrix products  59.7 us (27%)
  other arithmetic  57.5 us (26%)
  waiting for transfers between devices  30.4 us (14%)
  local copies, waits for them, and re-layouts  24.1 us (11%)
  blocking collectives  20 us (9%)
  starting transfers between devices  17.6 us (8%)
  between operations  10.8 us (5%)
    dot_general x12, matrix products, pair_head(): jnp.dot(hidden, w_out, preferred_element_type=jnp.float32)  48.9 us
    reduce_sum x12, other arithmetic, pair_head(): variance = jnp.mean(centred * centred, axis=-1, keepdims=True)  27.9 us
    pmax x1, blocking collectives, shards(): tm_score = lax.pmax(best_share, 'tile')  20 us
    reduce_sum x12, other arithmetic, pair_head(): row_mean = jnp.mean(values, axis=-1, keepdims=True)  18.9 us
    all_to_all x1, waiting for transfers between devices, shards(): lax.all_to_all(error_out, 'tile', split_axis=0, concat_axis=0, tiled=True)  16.5 us
    slice x1, local copies, waits for them, and re-layouts, shards(): pair_tiles[slot].reshape(row_count // block_rows, block_rows, pair_width)  8.89 us
    all_to_all x1, starting transfers between devices, shards(): lax.all_to_all(rows_out, 'tile', split_axis=0, concat_axis=0, tiled=True)  6.45 us
    dynamic_update_slice x24, local copies, waits for them, and re-layouts, shards(): lax.map(head_block, pair_tiles[slot].reshape(row_count // block_rows, blo...  5.96 us
  transfers between devices with their start and end apart: 4, of which 4 were waited for; matrix products, arithmetic and copies ran while one was open for 3% of the time, Pallas kernels for 0%

commit v1 on v0

v1 whole, which is shorter than its diff:
```python
import functools
import math

import jax
import jax.numpy as jnp
from jax import lax
from jax.experimental import pallas as pl
from jax.experimental.pallas import tpu as pltpu
from jax.sharding import PartitionSpec as P

EPS = 1e-05
F32 = jnp.float32
BF16 = jnp.bfloat16
LOG2E = math.log2(math.e)
NT = (((1,), (1,)), ((), ()))
HIGHEST = lax.Precision.HIGHEST
GROUP = 4
PAD = 8
VMEM_LIMIT = 50 * 1024 * 1024


def split_bf16(values):
    high = values.astype(BF16)
    return high, (values - high.astype(F32)).astype(BF16)


def own_slots(map_ref, base, slots):
    return [
        (map_ref[base + s, 0], map_ref[base + s, 1], map_ref[base + s, 2]) for s in range(slots)
    ]


def valid_row(resolved_ref, lengths_ref, member, block, side):
    start = block * side
    if not isinstance(start, int):
        start = pl.multiple_of(start, side)
    flags = resolved_ref[:, pl.ds(start, side)]
    here = lax.broadcasted_iota(jnp.int32, flags.shape, 0) == member
    flags = jnp.max(jnp.where(here, flags, 0), axis=0, keepdims=True)
    position = start + lax.broadcasted_iota(jnp.int32, (1, side), 1)
    return ((flags > 0) & (position < lengths_ref[member])).astype(F32)


def head_kernel(
    dims,
    map_ref,
    lengths_ref,
    flags_ref,
    resolved_ref,
    tiles_ref,
    gain_ref,
    w_in_ref,
    w_out_ref,
    w_head_ref,
    bias_ref,
    *rest,
):
    n_cplx, parts, cpx_dev, slots, side, width, hid, bins, rows_each = dims
    outs = rest[: n_cplx * parts]
    (
        tiles,
        first_w,
        second_w,
        bias_tile,
        sum_w,
        hidden,
        direct,
        spread,
        logits,
        sums,
        errors,
        tm_sums,
        order,
        sems,
    ) = rest[n_cplx * parts :]
    tile_index = lax.axis_index("tile")
    cplx_index = lax.axis_index("cplx")
    part_index = lax.rem(tile_index, parts)
    metas = own_slots(map_ref, (tile_index * n_cplx + cplx_index) * slots, slots)
    total = slots * side

    def slot_copy(s):
        return pltpu.make_async_copy(
            tiles_ref.at[s], tiles.at[pl.ds(s * side, side)], sems.at[s]
        )

    for s in range(slots):

        @pl.when(metas[s][0] >= 0)
        def _(s=s):
            slot_copy(s).start()

    count = jnp.int32(0)
    starts = []
    unroll = 8
    for s in range(slots):
        starts.append(count)
        member = jnp.maximum(metas[s][0], 0)
        base = jnp.maximum(metas[s][1], 0) * side
        limit = jnp.where(metas[s][0] >= 0, jnp.minimum(lengths_ref[member] - base, side), 0)
        limit = jnp.maximum(limit, 0)

        def step(g, cnt, s=s, member=member, base=base, limit=limit):
            for u in range(unroll):
                row = g * unroll + u
                order[cnt] = s * side + row
                keep = (flags_ref[member, base + row] > 0) & (row < limit)
                cnt = cnt + keep.astype(jnp.int32)
            return cnt

        count = lax.fori_loop(0, pl.cdiv(limit, unroll), step, count)
    batch = 2 * GROUP
    for u in range(2 * batch):
        order[count + u] = total

    w_in_t = jnp.transpose(w_in_ref[...].astype(F32)) * gain_ref[...]
    w_in_t = w_in_t - jnp.mean(w_in_t, axis=1, keepdims=True)
    head_t = jnp.transpose(w_head_ref[...].astype(F32))
    both = jnp.concatenate([w_in_t, head_t * LOG2E], axis=0)
    high, low = split_bf16(both)
    first_w[: hid + bins, :width] = high
    first_w[: hid + bins, width:] = low
    row_id = lax.broadcasted_iota(jnp.int32, (width, width), 0)
    col_id = lax.broadcasted_iota(jnp.int32, (width, width), 1)
    centring = jnp.where(row_id == col_id, 1.0, 0.0) - 1.0 / width
    first_w[hid + bins :, :width] = centring.astype(BF16)
    first_w[hid + bins :, width:] = jnp.zeros((width, width), BF16)
    second = lax.dot_general(head_t.astype(BF16), w_out_ref[...], NT, preferred_element_type=F32)
    second_w[...] = (second * LOG2E).astype(BF16)
    bias_tile[...] = jnp.transpose(jnp.broadcast_to(bias_ref[...] * LOG2E, (128, bins)))
    step_size = 31.0 / (bins - 2)
    centers = (lax.broadcasted_iota(jnp.int32, (1, bins), 1).astype(F32) + 0.5) * step_size
    sum_rows = [jnp.ones((1, bins), F32).astype(BF16), centers.astype(BF16)]
    for s in range(slots):
        length = lengths_ref[jnp.maximum(metas[s][0], 0)]
        clipped = jnp.full((1, bins), jnp.maximum(length, 19) - 15, jnp.int32).astype(F32)
        distance = 1.24 * jnp.exp(jnp.log(clipped) * (1.0 / 3.0)) - 1.8
        sum_rows.extend(split_bf16(1.0 / (1.0 + (centers / distance) ** 2)))
    extra = sum_w.shape[0] - len(sum_rows)
    if extra:
        sum_rows.append(jnp.zeros((extra, bins), BF16))
    sum_w[...] = jnp.concatenate([r.astype(F32) for r in sum_rows], axis=0).astype(BF16)

    lanes = GROUP * side

    def project(first_row, slot):
        rows = [tiles[order[first_row + u]] for u in range(GROUP)]
        pairs = jnp.concatenate(rows, axis=0)
        pairs = jnp.concatenate([pairs, pairs], axis=1)
        out = lax.dot_general(first_w[...], pairs, NT, preferred_element_type=F32)
        hidden[slot] = jnp.maximum(out[:hid].astype(BF16), 0)
        direct[slot] = out[hid : hid + bins]
        centred = out[hid + bins :]
        variance = jnp.sum(centred * centred, axis=0, keepdims=True) * (1.0 / width)
        spread[slot] = jnp.broadcast_to(lax.rsqrt(variance + EPS), (8, lanes))

    def combine(slot):
        change = jnp.dot(second_w[...], hidden[slot], preferred_element_type=F32)
        scale = spread[slot][:1]
        bias = jnp.concatenate([bias_tile[...]] * (lanes // 128), axis=1)
        logits[slot] = direct[slot] + bias + jnp.where(scale > 0, scale * change, 0.0)

    def reduce(first_row, slot):
        values = logits[slot]
        top = jnp.max(values, axis=0, keepdims=True)
        weights = jnp.exp2(values - top).astype(BF16)
        found = jnp.dot(sum_w[...], weights, preferred_element_type=F32)
        for u in range(GROUP):
            row = order[jnp.maximum(first_row + u, 0)]
            row = jnp.where(first_row + u >= 0, row, total)
            sums[row] = found[:, u * side : (u + 1) * side]

    def wait_slots(first_row, last_row, condition):
        for s in range(slots):

            @pl.when(condition(s))
            def _(s=s):
                slot_copy(s).wait()

    steps = pl.cdiv(count, batch)

    def loop(g, carry):
        row = g * batch
        for s in range(slots):
            begin = starts[s]

            @pl.when((metas[s][0] >= 0) & (begin // batch == g))
            def _(s=s):
                slot_copy(s).wait()

        project(row, 0)
        combine(1)
        reduce(row - 2 * GROUP, 0)
        project(row + GROUP, 1)
        combine(0)
        reduce(row - GROUP, 1)
        return carry

    lax.fori_loop(0, steps + 1, loop, 0)
    for s in range(slots):

        @pl.when((metas[s][0] >= 0) & (starts[s] // batch > steps))
        def _(s=s):
            slot_copy(s).wait()

    for s in range(slots):
        member = jnp.maximum(metas[s][0], 0)
        block_row = jnp.maximum(metas[s][1], 0)
        block_col = jnp.maximum(metas[s][2], 0)
        row_ok = valid_row(resolved_ref, lengths_ref, member, block_row, side)
        col_ok = valid_row(resolved_ref, lengths_ref, member, block_col, side)
        keep_row = lax.broadcasted_iota(jnp.int32, (8, side), 0) == 0
        outer = lax.dot_general(
            jnp.where(keep_row, row_ok, 0.0),
            jnp.where(keep_row, col_ok, 0.0),
            (((0,), (0,)), ((), ())),
            preferred_element_type=F32,
        )
        mass = sums[pl.ds(s * side, side), 0, :]
        inverse = 1.0 / mass
        expected = sums[pl.ds(s * side, side), 1, :] * inverse
        high = sums[pl.ds(s * side, side), 2 + 2 * s, :]
        low = sums[pl.ds(s * side, side), 3 + 2 * s, :]
        errors[s] = jnp.where(outer > 0, expected, 0.0)
        term = jnp.where(outer > 0, (high + low) * inverse, 0.0)
        tm_sums[s] = lax.dot_general(
            jnp.ones((PAD, side), F32), term, NT, preferred_element_type=F32, precision=HIGHEST
        )

    for shift in range(n_cplx):
        owner = lax.rem(cplx_index + shift, n_cplx)
        chosen = jnp.int32(0)
        for s in range(slots):
            hit = (metas[s][0] >= 0) & (metas[s][0] // cpx_dev == owner)
            chosen = jnp.where(hit, s, chosen)
        for part_shift in range(parts):
            part = lax.rem(part_index + part_shift, parts)
            out = outs[shift * parts + part_shift]
            first = pl.multiple_of(part * rows_each, rows_each)
            out[:rows_each] = errors[chosen, pl.ds(first, rows_each)]
            out[rows_each:] = tm_sums[chosen]


def place_kernel(dims, map_ref, *rest):
    n_cplx, parts, cpx_dev, slots, blocks, rows_each, side = dims
    pieces = rest[: n_cplx * parts]
    outs = rest[n_cplx * parts : n_cplx * parts + blocks]
    (tm_rows,) = rest[n_cplx * parts + blocks :]
    tile_index = lax.axis_index("tile")
    cplx_index = lax.axis_index("cplx")
    part_index = lax.rem(tile_index, parts)
    block_index = tile_index // parts
    body = cpx_dev * blocks * rows_each
    for out in outs:
        out[...] = jnp.zeros_like(out)
    tm_rows[...] = jnp.zeros_like(tm_rows)
    for shift in range(n_cplx):
        source = lax.rem(cplx_index + (n_cplx - shift), n_cplx)
        for part_shift in range(parts):
            part = lax.rem(part_index + (parts - part_shift), parts)
            device = (block_index * parts + part) * n_cplx + source
            piece = pieces[shift * parts + part_shift]
            member = jnp.int32(-1)
            block_row = jnp.int32(0)
            block_col = jnp.int32(0)
            for s, (k, r, q) in enumerate(own_slots(map_ref, device * slots, slots)):
                hit = (k >= 0) & (k // cpx_dev == cplx_index)
                member = jnp.where(hit, k - cplx_index * cpx_dev, member)
                block_row = jnp.where(hit, r, block_row)
                block_col = jnp.where(hit, q, block_col)
            offset = lax.rem(block_row - block_index + blocks, blocks)
            for b in range(blocks):

                @pl.when((member >= 0) & (offset == b))
                def _(b=b, piece=piece, member=member, block_col=block_col):
                    first = pl.multiple_of((member * blocks + block_col) * rows_each, 8)
                    outs[b][pl.ds(first, rows_each)] = piece[:rows_each]

            @pl.when(member >= 0)
            def _(piece=piece, member=member, block_row=block_row):
                row = member * blocks + block_row
                tm_rows[pl.ds(row, 1)] += piece[rows_each : rows_each + 1]

    for out in outs:
        out[body:] = tm_rows[...]


def finish_kernel(dims, lengths_ref, resolved_ref, *rest):
    parts, cpx_dev, blocks, rows_each, side = dims
    shares = rest[:blocks]
    map_out, error_out, score_out = rest[blocks:]
    tile_index = lax.axis_index("tile")
    cplx_index = lax.axis_index("cplx")
    part_index = lax.rem(tile_index, parts)
    block_index = tile_index // parts
    body = cpx_dev * blocks * rows_each
    tm_all = shares[0][body:]
    for share in shares[1:]:
        tm_all = tm_all + share[body:]
    for m in range(cpx_dev):
        member = cplx_index * cpx_dev + m
        masks = [valid_row(resolved_ref, lengths_ref, member, b, side) for b in range(blocks)]
        count = jnp.sum(functools.reduce(jnp.add, masks), axis=1, keepdims=True)
        row_sum = jnp.zeros((rows_each, side), F32)
        for q in range(blocks):
            rows = pl.ds((m * blocks + q) * rows_each, rows_each)
            block = shares[0][rows]
            for share in shares[1:]:
                block = block + share[rows]
            map_out[m, :, q * side : (q + 1) * side] = block
            row_sum = row_sum + block
        row_total = lax.dot_general(
            jnp.ones((8, side), F32), row_sum, NT, preferred_element_type=F32, precision=HIGHEST
        )[:1]
        best = jnp.zeros((1, side), F32)
        own_mask = jnp.zeros((1, side), F32)
        for b in range(blocks):
            denominator = jnp.maximum(masks[b] * count, 1.0)
            ratio = tm_all[m * blocks + b : m * blocks + b + 1] / denominator
            best = ratio if b == 0 else jnp.maximum(best, ratio)
            own_mask = jnp.where(block_index == b, masks[b], own_mask)
        own_mask = pltpu.roll(
            jnp.broadcast_to(own_mask, (8, side)),
            lax.rem(side - part_index * rows_each, side),
            axis=1,
        )[:1, :rows_each]
        error_out[m : m + 1, :] = row_total / jnp.maximum(own_mask * count, 1.0)
        score_out[m] = jnp.max(best)


def shards(pair_tiles, tile_map, lengths, resolved, ln_gain, w_in, w_out, w_head, head_bias):
    n_tile = lax.axis_size("tile")
    n_cplx = lax.axis_size("cplx")
    slots, side, _, width = pair_tiles.shape
    complexes, maxres = resolved.shape
    hid = w_in.shape[1]
    bins = w_head.shape[1]
    blocks = maxres // side
    cpx_dev = complexes // n_cplx
    rows_each = maxres // n_tile
    parts = side // rows_each
    smem = pl.BlockSpec(memory_space=pltpu.SMEM)
    vmem = pl.BlockSpec(memory_space=pltpu.VMEM)
    axes = ("tile", "cplx")
    sum_count = -(-(2 + 2 * slots) // 8) * 8
    lanes = GROUP * side

    def move(value, block_shift, part_shift, cplx_shift):
        pairs = []
        for t in range(n_tile):
            to_block = (t // parts + block_shift) % blocks
            to_part = (t % parts + part_shift) % parts
            for c in range(n_cplx):
                to = (to_block * parts + to_part) * n_cplx + (c + cplx_shift) % n_cplx
                pairs.append((t * n_cplx + c, to))
        return lax.ppermute(value, axes, pairs)

    piece = jax.ShapeDtypeStruct((rows_each + PAD, side), F32)
    pieces = pl.pallas_call(
        functools.partial(
            head_kernel, (n_cplx, parts, cpx_dev, slots, side, width, hid, bins, rows_each)
        ),
        out_shape=[piece] * (n_cplx * parts),
        in_specs=[smem, smem, smem, vmem, pl.BlockSpec(memory_space=pl.ANY)] + [vmem] * 5,
        out_specs=[vmem] * (n_cplx * parts),
        scratch_shapes=[
            pltpu.VMEM((slots * side + 8, side, width), BF16),
            pltpu.VMEM((hid + bins + width, 2 * width), BF16),
            pltpu.VMEM((bins, hid), BF16),
            pltpu.VMEM((bins, 128), F32),
            pltpu.VMEM((sum_count, bins), BF16),
            pltpu.VMEM((2, hid, lanes), BF16),
            pltpu.VMEM((2, bins, lanes), F32),
            pltpu.VMEM((2, 8, lanes), F32),
            pltpu.VMEM((2, bins, lanes), F32),
            pltpu.VMEM((slots * side + 8, sum_count, side), F32),
            pltpu.VMEM((slots, side, side), F32),
            pltpu.VMEM((slots, PAD, side), F32),
            pltpu.SMEM((slots * side + 64,), jnp.int32),
            pltpu.SemaphoreType.DMA((slots,)),
        ],
        compiler_params=pltpu.CompilerParams(vmem_limit_bytes=VMEM_LIMIT),
    )(
        tile_map,
        lengths,
        resolved,
        resolved,
        pair_tiles,
        ln_gain.reshape(1, width),
        w_in,
        w_out,
        w_head,
        head_bias.reshape(1, bins),
    )
    moved = []
    for shift in range(n_cplx):
        for part_shift in range(parts):
            value = pieces[shift * parts + part_shift]
            moved.append(move(value, 0, part_shift, shift) if shift or part_shift else value)

    tm_pad = -(-(cpx_dev * blocks) // 8) * 8
    share = jax.ShapeDtypeStruct((cpx_dev * blocks * rows_each + tm_pad, side), F32)
    shares = pl.pallas_call(
        functools.partial(
            place_kernel, (n_cplx, parts, cpx_dev, slots, blocks, rows_each, side)
        ),
        out_shape=[share] * blocks,
        in_specs=[smem] + [vmem] * len(moved),
        out_specs=[vmem] * blocks,
        scratch_shapes=[pltpu.VMEM((tm_pad, side), F32)],
    )(tile_map, *moved)
    arrived = [move(shares[b], b, 0, 0) if b else shares[b] for b in range(blocks)]

    return pl.pallas_call(
        functools.partial(finish_kernel, (parts, cpx_dev, blocks, rows_each, side)),
        out_shape=[
            jax.ShapeDtypeStruct((cpx_dev, rows_each, maxres), F32),
            jax.ShapeDtypeStruct((cpx_dev, rows_each), F32),
            jax.ShapeDtypeStruct((cpx_dev,), F32),
        ],
        in_specs=[smem, vmem] + [vmem] * blocks,
        out_specs=[vmem, vmem, smem],
    )(lengths, resolved, *arrived)


def solution(mesh):
    placed = (P(("tile", "cplx"), None, None, None), P(), P(), P(), P(), P(), P(), P(), P())
    return jax.shard_map(
        shards,
        mesh=mesh,
        in_specs=placed,
        out_specs=(P("cplx", "tile", None), P("cplx", "tile"), P("cplx")),
        check_vma=False,
    )
```

time: 223 us -> 77.5 us (0.35)
  the two profiles are of different devices: /device:TPU:0 before, /device:TPU:9 now
where the time goes in v1:
time: 77.5 us; the launch traced here: 77.4 us
  Pallas kernels  32.5 us (42%)
  starting transfers between devices  21 us (27%)
  waiting for transfers between devices  15.2 us (20%)
  local copies, waits for them, and re-layouts  7.93 us (10%)
    pallas_call x1, Pallas kernels, shards(): pl.pallas_call(functools.partial(head_kernel, (n_cplx, parts, cpx_dev, sl...  27.8 us
    ppermute x10, starting transfers between devices, move(): return lax.ppermute(value, axes, pairs)  21 us
    ppermute x10, waiting for transfers between devices, move(): return lax.ppermute(value, axes, pairs)  15.2 us
    unnamed x38, local copies, waits for them, and re-layouts  7.93 us
    pallas_call x1, Pallas kernels, shards(): pl.pallas_call(functools.partial(place_kernel, (n_cplx, parts, cpx_dev, s...  2.81 us
    pallas_call x1, Pallas kernels, shards(): pl.pallas_call(functools.partial(finish_kernel, (parts, cpx_dev, blocks,...  1.88 us
  transfers between devices with their start and end apart: 10, of which 6 were waited for; matrix products, arithmetic and copies ran while one was open for 0% of the time, Pallas kernels for 0%

profile of v1, /device:TPU:9, one launch (start us, length us, event | category | flops | bytes accessed | tf_op | source)
XLA Modules:
  0.0 77.4 jit_solution(5817496355898015381)
XLA Ops:
  0.6 0.8 %copy.13.w_head_ref = bf16[128,64]{1,0:T(8,128)(2,1)S(1)} copy(bf16[128,64]{0,1:T(8,128)(2,1)} %param.16) | data formatting | bytes 32768 | tf_op args[7]
  1.5 0.8 %copy.14.map_ref = s32[96,3]{1,0:T(8,128)S(1)} copy(s32[96,3]{0,1:T(4,128)} %param.10) | data formatting | bytes 2304 | tf_op args[1]
  2.3 0.0 copy-start.1
  2.3 0.9 %copy-done.1 = bf16[128,512]{1,0:T(8,128)(2,1)S(1)} copy-done((bf16[128,512]{1,0:T(8,128)(2,1)S(1)}, bf16[128,512]{1,0:T(8,128)(2,1)}, u32[]{:S(2)}) %copy-start.1) | copy-done | bytes 131096
  3.2 0.9 %copy-done.2 = bf16[512,128]{1,0:T(8,128)(2,1)S(1)} copy-done((bf16[512,128]{1,0:T(8,128)(2,1)S(1)}, bf16[512,128]{1,0:T(8,128)(2,1)}, u32[]{:S(2)}) %copy-start.2) | copy-done | bytes 131096
  4.1 0.7 copy-done.3
  4.8 0.7 copy-done.5
  5.4 0.7 copy-done.6
  6.1 0.7 copy-done.7
  6.7 27.8 %shard_map.112 = (f32[72,128]{1,0:T(8,128)S(1)}, f32[72,128]{1,0:T(8,128)S(1)}, f32[72,128]{1,0:T(8,128)S(1)}, f32[72,128]{1,0:T(8,128)S(1)}, f32[72,128]{1,0:T(...) custom-call(s32[96,3]{1,0:T(8,128)S(1)} %copy.14.map_ref, s32[4]{0:T(128)S(1)} %copy-done.5, ...), custom_call_target="tpu_custom_call" | custom-call | tf_op jit(solution)/shard_map/pallas_call | solution.py:359
  34.6 0.6 copy-done.4
  35.2 1.2 %collective-permute-start = (f32[72,128]{1,0:T(8,128)S(1)}, f32[72,128]{1,0:T(8,128)S(1)}, u32[]{:S(2)}, u32[]{:S(2)}) collective-permute-start(f32[72,128]{1,0:T(8,128)S(1)} %get-tuple-element.16), channel_id=1, source_target_pairs={{0,4},{1,5},{2,6},{3,7},{4,0},{5,1},{6,2},{7,3},{8,12},{9,13},{10,... | collective-permute-start | bytes 110600 | tf_op jit(solution)/shard_map/ppermute | solution.py:356
  36.4 0.0 collective-permute-start.1
  36.4 14.4 %collective-permute-start.2 = (f32[72,128]{1,0:T(8,128)S(1)}, f32[72,128]{1,0:T(8,128)S(1)}, u32[]{:S(2)}, u32[]{:S(2)}) collective-permute-start(f32[72,128]{1,0:T(8,128)S(1)} %get-tuple-element.18), channel_id=1, source_target_pairs={{0,5},{1,6},{2,7},{3,4},{4,1},{5,2},{6,3},{7,0},{8,13},{9,14},{10,... | collective-permute-start | bytes 110600 | tf_op jit(solution)/shard_map/ppermute | solution.py:356
  50.9 1.2 %collective-permute-start.4 = (f32[72,128]{1,0:T(8,128)S(1)}, f32[72,128]{1,0:T(8,128)S(1)}, u32[]{:S(2)}, u32[]{:S(2)}) collective-permute-start(f32[72,128]{1,0:T(8,128)S(1)} %get-tuple-element.20), channel_id=1, source_target_pairs={{0,6},{1,7},{2,4},{3,5},{4,2},{5,3},{6,0},{7,1},{8,14},{9,15},{10,... | collective-permute-start | bytes 110600 | tf_op jit(solution)/shard_map/ppermute | solution.py:356
  52.0 0.0 collective-permute-done.rest_1_
  52.0 0.0 collective-permute-start.5
  52.1 0.0 collective-permute-done.1.rest_2_
  52.1 1.7 %collective-permute-start.6 = (f32[72,128]{1,0:T(8,128)S(1)}, f32[72,128]{1,0:T(8,128)S(1)}, u32[]{:S(2)}, u32[]{:S(2)}) collective-permute-start(f32[72,128]{1,0:T(8,128)S(1)} %get-tuple-element.22), channel_id=1, source_target_pairs={{0,7},{1,4},{2,5},{3,6},{4,3},{5,0},{6,1},{7,2},{8,15},{9,12},{10,... | collective-permute-start | bytes 110600 | tf_op jit(solution)/shard_map/ppermute | solution.py:356
  53.8 0.7 collective-permute-done.4.rest_5_
  54.6 1.2 %collective-permute-done.5.rest_6_ = f32[72,128]{1,0:T(8,128)S(1)} collective-permute-done((f32[72,128]{1,0:T(8,128)S(1)}, f32[72,128]{1,0:T(8,128)S(1)}, u32[]{:S(2)}, u32[]{:S(2)}) %collective-permute-start.5) | collective-permute-done | bytes 36896 | tf_op jit(solution)/shard_map/ppermute | solution.py:356
  55.7 1.3 %collective-permute-done.6.rest_7_ = f32[72,128]{1,0:T(8,128)S(1)} collective-permute-done((f32[72,128]{1,0:T(8,128)S(1)}, f32[72,128]{1,0:T(8,128)S(1)}, u32[]{:S(2)}, u32[]{:S(2)}) %collective-permute-start.6) | collective-permute-done | bytes 36896 | tf_op jit(solution)/shard_map/ppermute | solution.py:356
  57.1 0.6 copy-done.17
  57.6 2.8 %shard_map.113 = (f32[264,128]{1,0:T(8,128)}, f32[264,128]{1,0:T(8,128)}, f32[264,128]{1,0:T(8,128)}, f32[264,128]{1,0:T(8,128)}) custom-call(s32[96,3]{1,0:T(8,128)} %copy-done, f32[72,128]{1,0:T(8,128)} %copy-done.4, f32[72,128]{1,0:T(8,128)} %copy-done.11, f32[72,128]{1,0:T(8,128)} %copy-done.12, f32[72,128]{1,0:T(8,128)} %copy-done.13, ...), custom_call_target="tpu_custom_call" | custom-call | tf_op jit(solution)/shard_map/pallas_call | solution.py:403
  60.4 1.2 %collective-permute-start.7 = (f32[264,128]{1,0:T(8,128)}, f32[264,128]{1,0:T(8,128)S(1)}, u32[]{:S(2)}, u32[]{:S(2)}) collective-permute-start(f32[264,128]{1,0:T(8,128)} %get-tuple-element.24), channel_id=1, source_target_pairs={{0,8},{1,9},{2,10},{3,11},{4,12},{5,13},{6,14},{7,15},{8,16},{9,17... | collective-permute-start | bytes 405512 | tf_op jit(solution)/shard_map/ppermute | solution.py:356
  61.6 0.3 collective-permute-start.8
  61.8 1.0 %collective-permute-start.9 = (f32[264,128]{1,0:T(8,128)}, f32[264,128]{1,0:T(8,128)S(1)}, u32[]{:S(2)}, u32[]{:S(2)}) collective-permute-start(f32[264,128]{1,0:T(8,128)} %get-tuple-element.26), channel_id=1, source_target_pairs={{0,24},{1,25},{2,26},{3,27},{4,28},{5,29},{6,30},{7,31},{8,0},{9,1... | collective-permute-start | bytes 405512 | tf_op jit(solution)/shard_map/ppermute | solution.py:356
  62.8 3.4 %collective-permute-done.7.rest_1_ = f32[264,128]{1,0:T(8,128)S(1)} collective-permute-done((f32[264,128]{1,0:T(8,128)}, f32[264,128]{1,0:T(8,128)S(1)}, u32[]{:S(2)}, u32[]{:S(2)}) %collective-permute-start.7) | collective-permute-done | bytes 135200 | tf_op jit(solution)/shard_map/ppermute | solution.py:356
  66.2 7.4 %collective-permute-done.8.rest_2_ = f32[264,128]{1,0:T(8,128)S(1)} collective-permute-done((f32[264,128]{1,0:T(8,128)}, f32[264,128]{1,0:T(8,128)S(1)}, u32[]{:S(2)}, u32[]{:S(2)}) %collective-permute-start.8) | collective-permute-done | bytes 135200 | tf_op jit(solution)/shard_map/ppermute | solution.py:356
  73.6 1.2 %collective-permute-done.9.rest_3_ = f32[264,128]{1,0:T(8,128)S(1)} collective-permute-done((f32[264,128]{1,0:T(8,128)}, f32[264,128]{1,0:T(8,128)S(1)}, u32[]{:S(2)}, u32[]{:S(2)}) %collective-permute-start.9) | collective-permute-done | bytes 135200 | tf_op jit(solution)/shard_map/ppermute | solution.py:356
  74.9 0.6 copy-done.10
  75.5 1.9 %shard_map.114 = (f32[1,64,512]{2,1,0:T(8,128)}, f32[1,64]{1,0:T(1,128)}, f32[1]{0:T(128)}) custom-call(s32[4]{0:T(128)} %lengths_ref.3, s32[4,512]{1,0:T(4,128)} %resolved_ref.3, f32[264,128]{1,0:T(8,128)} %get-tuple-element.23.rest_0_, f32[264,128]{1,0:T(8,128)} %copy-done.8, f32[264,128]{1,0:T(8,128)} %copy-done.9, f32[264,128]{1,0:T(8,128)} %copy-done.10), custom_call_target="tpu_custom_call" | custom-call | tf_op jit(solution)/shard_map/pallas_call | solution.py:414
  (29 shorter events, 0.1 us)
Async XLA Ops:
  2.2 54.8 %copy-start = (s32[96,3]{1,0:T(8,128)}, s32[96,3]{1,0:T(8,128)S(1)}, u32[]{:S(2)}) copy-start(s32[96,3]{1,0:T(8,128)S(1)} %copy.14.map_ref) | copy-start | bytes 3460
  2.3 0.9 %copy-start.1 = (bf16[128,512]{1,0:T(8,128)(2,1)S(1)}, bf16[128,512]{1,0:T(8,128)(2,1)}, u32[]{:S(2)}) copy-start(bf16[128,512]{1,0:T(8,128)(2,1)} %w_in_ref.1) | copy-start | bytes 393220
  3.2 0.9 %copy-start.2 = (bf16[512,128]{1,0:T(8,128)(2,1)S(1)}, bf16[512,128]{1,0:T(8,128)(2,1)}, u32[]{:S(2)}) copy-start(bf16[512,128]{1,0:T(8,128)(2,1)} %w_out_ref.1) | copy-start | bytes 393220
  4.1 0.7 copy-start.3
  4.8 0.7 copy-start.5
  5.4 0.7 copy-start.6
  6.1 0.7 copy-start.7
  34.6 0.6 copy-start.4
  35.2 16.9 %collective-permute-start = (f32[72,128]{1,0:T(8,128)S(1)}, f32[72,128]{1,0:T(8,128)S(1)}, u32[]{:S(2)}, u32[]{:S(2)}) collective-permute-start(f32[72,128]{1,0:T(8,128)S(1)} %get-tuple-element.16), channel_id=1, source_target_pairs={{0,4},{1,5},{2,6},{3,7},{4,0},{5,1},{6,2},{7,3},{8,12},{9,13},{10,... | collective-permute-start | bytes 110600 | tf_op jit(solution)/shard_map/ppermute | solution.py:356
  36.4 15.6 %collective-permute-start.1 = (f32[72,128]{1,0:T(8,128)S(1)}, f32[72,128]{1,0:T(8,128)S(1)}, u32[]{:S(2)}, u32[]{:S(2)}) collective-permute-start(f32[72,128]{1,0:T(8,128)S(1)} %get-tuple-element.17), channel_id=1, source_target_pairs={{0,1},{1,2},{2,3},{3,0},{4,5},{5,6},{6,7},{7,4},{8,9},{9,10},{10,1... | collective-permute-start | bytes 110600 | tf_op jit(solution)/shard_map/ppermute | solution.py:356
  36.4 17.4 %collective-permute-start.2 = (f32[72,128]{1,0:T(8,128)S(1)}, f32[72,128]{1,0:T(8,128)S(1)}, u32[]{:S(2)}, u32[]{:S(2)}) collective-permute-start(f32[72,128]{1,0:T(8,128)S(1)} %get-tuple-element.18), channel_id=1, source_target_pairs={{0,5},{1,6},{2,7},{3,4},{4,1},{5,2},{6,3},{7,0},{8,13},{9,14},{10,... | collective-permute-start | bytes 110600 | tf_op jit(solution)/shard_map/ppermute | solution.py:356
  50.9 3.0 %collective-permute-start.3 = (f32[72,128]{1,0:T(8,128)S(1)}, f32[72,128]{1,0:T(8,128)S(1)}, u32[]{:S(2)}, u32[]{:S(2)}) collective-permute-start(f32[72,128]{1,0:T(8,128)S(1)} %get-tuple-element.19), channel_id=1, source_target_pairs={{0,2},{1,3},{2,0},{3,1},{4,6},{5,7},{6,4},{7,5},{8,10},{9,11},{10,... | collective-permute-start | bytes 110600 | tf_op jit(solution)/shard_map/ppermute | solution.py:356
  50.9 3.7 %collective-permute-start.4 = (f32[72,128]{1,0:T(8,128)S(1)}, f32[72,128]{1,0:T(8,128)S(1)}, u32[]{:S(2)}, u32[]{:S(2)}) collective-permute-start(f32[72,128]{1,0:T(8,128)S(1)} %get-tuple-element.20), channel_id=1, source_target_pairs={{0,6},{1,7},{2,4},{3,5},{4,2},{5,3},{6,0},{7,1},{8,14},{9,15},{10,... | collective-permute-start | bytes 110600 | tf_op jit(solution)/shard_map/ppermute | solution.py:356
  52.0 5.0 %copy-start.11 = (f32[72,128]{1,0:T(8,128)}, f32[72,128]{1,0:T(8,128)S(1)}, u32[]{:S(2)}) copy-start(f32[72,128]{1,0:T(8,128)S(1)} %collective-permute-done.rest_1_) | copy-start | bytes 110596
  52.0 3.7 %collective-permute-start.5 = (f32[72,128]{1,0:T(8,128)S(1)}, f32[72,128]{1,0:T(8,128)S(1)}, u32[]{:S(2)}, u32[]{:S(2)}) collective-permute-start(f32[72,128]{1,0:T(8,128)S(1)} %get-tuple-element.21), channel_id=1, source_target_pairs={{0,3},{1,0},{2,1},{3,2},{4,7},{5,4},{6,5},{7,6},{8,11},{9,8},{10,9... | collective-permute-start | bytes 110600 | tf_op jit(solution)/shard_map/ppermute | solution.py:356
  52.1 5.0 %copy-start.12 = (f32[72,128]{1,0:T(8,128)}, f32[72,128]{1,0:T(8,128)S(1)}, u32[]{:S(2)}) copy-start(f32[72,128]{1,0:T(8,128)S(1)} %collective-permute-done.1.rest_2_) | copy-start | bytes 110596
  52.1 4.9 %collective-permute-start.6 = (f32[72,128]{1,0:T(8,128)S(1)}, f32[72,128]{1,0:T(8,128)S(1)}, u32[]{:S(2)}, u32[]{:S(2)}) collective-permute-start(f32[72,128]{1,0:T(8,128)S(1)} %get-tuple-element.22), channel_id=1, source_target_pairs={{0,7},{1,4},{2,5},{3,6},{4,3},{5,0},{6,1},{7,2},{8,15},{9,12},{10,... | collective-permute-start | bytes 110600 | tf_op jit(solution)/shard_map/ppermute | solution.py:356
  53.8 3.2 %copy-start.13 = (f32[72,128]{1,0:T(8,128)}, f32[72,128]{1,0:T(8,128)S(1)}, u32[]{:S(2)}) copy-start(f32[72,128]{1,0:T(8,128)S(1)} %collective-permute-done.2.rest_3_) | copy-start | bytes 110596
  53.8 3.2 %copy-start.14 = (f32[72,128]{1,0:T(8,128)}, f32[72,128]{1,0:T(8,128)S(1)}, u32[]{:S(2)}) copy-start(f32[72,128]{1,0:T(8,128)S(1)} %collective-permute-done.3.rest_4_) | copy-start | bytes 110596
  54.6 2.5 %copy-start.15 = (f32[72,128]{1,0:T(8,128)}, f32[72,128]{1,0:T(8,128)S(1)}, u32[]{:S(2)}) copy-start(f32[72,128]{1,0:T(8,128)S(1)} %collective-permute-done.4.rest_5_) | copy-start | bytes 110596
  55.7 1.3 %copy-start.16 = (f32[72,128]{1,0:T(8,128)}, f32[72,128]{1,0:T(8,128)S(1)}, u32[]{:S(2)}) copy-start(f32[72,128]{1,0:T(8,128)S(1)} %collective-permute-done.5.rest_6_) | copy-start | bytes 110596
  57.0 0.6 copy-start.17
  60.4 5.8 %collective-permute-start.7 = (f32[264,128]{1,0:T(8,128)}, f32[264,128]{1,0:T(8,128)S(1)}, u32[]{:S(2)}, u32[]{:S(2)}) collective-permute-start(f32[264,128]{1,0:T(8,128)} %get-tuple-element.24), channel_id=1, source_target_pairs={{0,8},{1,9},{2,10},{3,11},{4,12},{5,13},{6,14},{7,15},{8,16},{9,17... | collective-permute-start | bytes 405512 | tf_op jit(solution)/shard_map/ppermute | solution.py:356
  61.6 12.0 %collective-permute-start.8 = (f32[264,128]{1,0:T(8,128)}, f32[264,128]{1,0:T(8,128)S(1)}, u32[]{:S(2)}, u32[]{:S(2)}) collective-permute-start(f32[264,128]{1,0:T(8,128)} %get-tuple-element.25), channel_id=1, source_target_pairs={{0,16},{1,17},{2,18},{3,19},{4,20},{5,21},{6,22},{7,23},{8,24},{9,... | collective-permute-start | bytes 405512 | tf_op jit(solution)/shard_map/ppermute | solution.py:356
  61.8 13.0 %collective-permute-start.9 = (f32[264,128]{1,0:T(8,128)}, f32[264,128]{1,0:T(8,128)S(1)}, u32[]{:S(2)}, u32[]{:S(2)}) collective-permute-start(f32[264,128]{1,0:T(8,128)} %get-tuple-element.26), channel_id=1, source_target_pairs={{0,24},{1,25},{2,26},{3,27},{4,28},{5,29},{6,30},{7,31},{8,0},{9,1... | collective-permute-start | bytes 405512 | tf_op jit(solution)/shard_map/ppermute | solution.py:356
  66.2 8.6 %copy-start.8 = (f32[264,128]{1,0:T(8,128)}, f32[264,128]{1,0:T(8,128)S(1)}, u32[]{:S(2)}) copy-start(f32[264,128]{1,0:T(8,128)S(1)} %collective-permute-done.7.rest_1_) | copy-start | bytes 405508
  73.6 1.2 %copy-start.9 = (f32[264,128]{1,0:T(8,128)}, f32[264,128]{1,0:T(8,128)S(1)}, u32[]{:S(2)}) copy-start(f32[264,128]{1,0:T(8,128)S(1)} %collective-permute-done.8.rest_2_) | copy-start | bytes 405508
  74.9 0.6 copy-start.10

commit v2 on v1

--- a/solution.py
+++ b/solution.py
@@ -15,8 +15,11 @@
 NT = (((1,), (1,)), ((), ()))
 HIGHEST = lax.Precision.HIGHEST
 GROUP = 4
+UNROLL = 4
+MXUS = 2
+CHUNK = 64
 PAD = 8
-VMEM_LIMIT = 50 * 1024 * 1024
+VMEM_LIMIT = 67043328
 
 
 def split_bf16(values):
@@ -26,7 +29,7 @@
 
 def own_slots(map_ref, base, slots):
     return [
-        (map_ref[base + s, 0], map_ref[base + s, 1], map_ref[base + s, 2]) for s in range(slots)
+        (map_ref[0, base + s], map_ref[1, base + s], map_ref[2, base + s]) for s in range(slots)
     ]
 
 
@@ -41,7 +44,7 @@
     return ((flags > 0) & (position < lengths_ref[member])).astype(F32)
 
 
-def head_kernel(
+def head_body(
     dims,
     map_ref,
     lengths_ref,
@@ -62,17 +65,21 @@
         first_w,
         second_w,
         bias_tile,
-        sum_w,
+        center_tile,
+        tm_tile,
         hidden,
         direct,
         spread,
         logits,
-        sums,
+        found_error,
+        found_term,
         errors,
         tm_sums,
         order,
         sems,
+        *accs,
     ) = rest[n_cplx * parts :]
+    accs = [accs[m :: MXUS] for m in range(MXUS)]
     tile_index = lax.axis_index("tile")
     cplx_index = lax.axis_index("cplx")
     part_index = lax.rem(tile_index, parts)
@@ -109,13 +116,13 @@
             return cnt
 
         count = lax.fori_loop(0, pl.cdiv(limit, unroll), step, count)
-    batch = 2 * GROUP
-    for u in range(2 * batch):
+    batch = UNROLL * GROUP
+    for u in range(4 * GROUP + batch):
         order[count + u] = total
 
     w_in_t = jnp.transpose(w_in_ref[...].astype(F32)) * gain_ref[...]
     w_in_t = w_in_t - jnp.mean(w_in_t, axis=1, keepdims=True)
-    head_t = jnp.transpose(w_head_ref[...].astype(F32))
+    head_t = w_head_ref[...].astype(F32)
     both = jnp.concatenate([w_in_t, head_t * LOG2E], axis=0)
     high, low = split_bf16(both)
     first_w[: hid + bins, :width] = high
@@ -125,78 +132,120 @@
     centring = jnp.where(row_id == col_id, 1.0, 0.0) - 1.0 / width
     first_w[hid + bins :, :width] = centring.astype(BF16)
     first_w[hid + bins :, width:] = jnp.zeros((width, width), BF16)
-    second = lax.dot_general(head_t.astype(BF16), w_out_ref[...], NT, preferred_element_type=F32)
-    second_w[...] = (second * LOG2E).astype(BF16)
+    left = jnp.concatenate([head_t, jnp.zeros_like(head_t)], axis=1).astype(BF16)
+    for k in range(hid // (2 * width)):
+        part = w_out_ref[k * 2 * width : (k + 1) * 2 * width]
+        right = jnp.concatenate([part, jnp.zeros_like(part)], axis=1)
+        pltpu.matmul_push_rhs(right, 0, k % MXUS, transpose=True)
+        acc = accs[k % MXUS][0]
+        pltpu.matmul_acc_lhs(acc, left, 0)
+        second = pltpu.matmul_pop(acc) * LOG2E
+        second_w[:, k * 2 * width : (k + 1) * 2 * width] = second.astype(BF16)
     bias_tile[...] = jnp.transpose(jnp.broadcast_to(bias_ref[...] * LOG2E, (128, bins)))
     step_size = 31.0 / (bins - 2)
-    centers = (lax.broadcasted_iota(jnp.int32, (1, bins), 1).astype(F32) + 0.5) * step_size
-    sum_rows = [jnp.ones((1, bins), F32).astype(BF16), centers.astype(BF16)]
+    bin_id = lax.broadcasted_iota(jnp.int32, (bins, 128), 0)
+    centers = (bin_id.astype(F32) + 0.5) * step_size
+    center_tile[...] = centers
     for s in range(slots):
         length = lengths_ref[jnp.maximum(metas[s][0], 0)]
-        clipped = jnp.full((1, bins), jnp.maximum(length, 19) - 15, jnp.int32).astype(F32)
+        clipped = jnp.full((bins, 128), jnp.maximum(length, 19) - 15, jnp.int32).astype(F32)
         distance = 1.24 * jnp.exp(jnp.log(clipped) * (1.0 / 3.0)) - 1.8
-        sum_rows.extend(split_bf16(1.0 / (1.0 + (centers / distance) ** 2)))
-    extra = sum_w.shape[0] - len(sum_rows)
-    if extra:
-        sum_rows.append(jnp.zeros((extra, bins), BF16))
-    sum_w[...] = jnp.concatenate([r.astype(F32) for r in sum_rows], axis=0).astype(BF16)
+        tm_tile[s] = 1.0 / (1.0 + (centers / distance) ** 2)
 
     lanes = GROUP * side
-
-    def project(first_row, slot):
-        rows = [tiles[order[first_row + u]] for u in range(GROUP)]
-        pairs = jnp.concatenate(rows, axis=0)
-        pairs = jnp.concatenate([pairs, pairs], axis=1)
-        out = lax.dot_general(first_w[...], pairs, NT, preferred_element_type=F32)
-        hidden[slot] = jnp.maximum(out[:hid].astype(BF16), 0)
-        direct[slot] = out[hid : hid + bins]
-        centred = out[hid + bins :]
-        variance = jnp.sum(centred * centred, axis=0, keepdims=True) * (1.0 / width)
-        spread[slot] = jnp.broadcast_to(lax.rsqrt(variance + EPS), (8, lanes))
-
-    def combine(slot):
-        change = jnp.dot(second_w[...], hidden[slot], preferred_element_type=F32)
-        scale = spread[slot][:1]
-        bias = jnp.concatenate([bias_tile[...]] * (lanes // 128), axis=1)
-        logits[slot] = direct[slot] + bias + jnp.where(scale > 0, scale * change, 0.0)
-
-    def reduce(first_row, slot):
-        values = logits[slot]
-        top = jnp.max(values, axis=0, keepdims=True)
-        weights = jnp.exp2(values - top).astype(BF16)
-        found = jnp.dot(sum_w[...], weights, preferred_element_type=F32)
+    half = lanes // MXUS
+    depth = 2 * width
+    chunks = (hid + bins + width) // CHUNK
+
+    def push_pairs(first_row):
+        for m in range(MXUS):
+            rows = [tiles[order[first_row + m * (GROUP // MXUS) + u]] for u in range(GROUP // MXUS)]
+            pairs = jnp.concatenate(rows, axis=0)
+            pairs = jnp.concatenate([pairs, pairs], axis=1)
+            pltpu.matmul_push_rhs(pairs, 0, m, transpose=True)
+
+    def take(slot, chunk, m, variance):
+        value = pltpu.matmul_pop(accs[m][chunk])
+        at = chunk * CHUNK
+        cols = slice(m * half, (m + 1) * half)
+        if at < hid:
+            hidden[slot, at : at + CHUNK, cols] = jnp.maximum(value.astype(BF16), 0)
+        elif at < hid + bins:
+            direct[slot, at - hid : at - hid + CHUNK, cols] = value
+        else:
+            part = jnp.sum((value * value).reshape(CHUNK // 8, 8, half), axis=0)
+            variance[m] = part if variance[m] is None else variance[m] + part
+
+    def weigh(first_row, slot):
         for u in range(GROUP):
             row = order[jnp.maximum(first_row + u, 0)]
             row = jnp.where(first_row + u >= 0, row, total)
-            sums[row] = found[:, u * side : (u + 1) * side]
-
-    def wait_slots(first_row, last_row, condition):
+            values = logits[slot, :, u * side : (u + 1) * side]
+            top = jnp.max(values, axis=0, keepdims=True)
+            weights = jnp.exp2(values - top)
+            inverse = 1.0 / jnp.sum(weights, axis=0, keepdims=True)
+            expected = jnp.sum(weights * center_tile[...], axis=0, keepdims=True)
+            term = jnp.sum(weights * tm_tile[row // side], axis=0, keepdims=True)
+            found_error[pl.ds(row, 1)] = expected * inverse
+            found_term[pl.ds(row, 1)] = term * inverse
+
+    def stage(group, slot):
+        other = 1 - slot
+        variance = [None] * MXUS
+        for chunk in range(chunks):
+            for m in range(MXUS):
+                left = first_w[chunk * CHUNK : (chunk + 1) * CHUNK]
+                pltpu.matmul_acc_lhs(accs[m][chunk], left, 0 if chunk == 0 else None)
+            if chunk == 1 or chunk == 4:
+                k = chunk // 4
+                for m in range(MXUS):
+                    right = hidden[other, k * depth : (k + 1) * depth, m * half : (m + 1) * half]
+                    pltpu.matmul_push_rhs(right, k, m)
+            if chunk >= 1:
+                for m in range(MXUS):
+                    take(slot, chunk - 1, m, variance)
+        for k in range(hid // depth):
+            for m in range(MXUS):
+                pltpu.matmul_acc_lhs(accs[m][chunks], second_w[:, k * depth : (k + 1) * depth], k)
+            if k == 0:
+                push_pairs((group + 1) * GROUP)
+        weigh((group - 2) * GROUP, slot)
+        for m in range(MXUS):
+            take(slot, chunks - 1, m, variance)
+            spread_now = jnp.sum(variance[m], axis=0, keepdims=True) * (1.0 / width)
+            spread[slot, :, m * half : (m + 1) * half] = jnp.broadcast_to(
+                lax.rsqrt(spread_now + EPS), (8, half)
+            )
+            cols = slice(m * half, (m + 1) * half)
+            scale = spread[other, :1, cols]
+            change = pltpu.matmul_pop(accs[m][chunks])
+            bias = jnp.concatenate([bias_tile[...]] * (half // 128), axis=1)
+            values = direct[other, :, cols] + bias + jnp.where(scale > 0, scale * change, 0.0)
+            logits[other, :, cols] = values
+
+    groups = pl.cdiv(count, GROUP)
+
+    def wait_for(g):
         for s in range(slots):
 
-            @pl.when(condition(s))
+            @pl.when((metas[s][0] >= 0) & (starts[s] // batch == g))
             def _(s=s):
                 slot_copy(s).wait()
 
-    steps = pl.cdiv(count, batch)
+    wait_for(0)
+    push_pairs(0)
 
     def loop(g, carry):
-        row = g * batch
-        for s in range(slots):
-            begin = starts[s]
-
-            @pl.when((metas[s][0] >= 0) & (begin // batch == g))
-            def _(s=s):
-                slot_copy(s).wait()
-
-        project(row, 0)
-        combine(1)
-        reduce(row - 2 * GROUP, 0)
-        project(row + GROUP, 1)
-        combine(0)
-        reduce(row - GROUP, 1)
+        wait_for(g + 1)
+        for u in range(UNROLL):
+            stage(g * UNROLL + u, u % 2)
         return carry
 
-    lax.fori_loop(0, steps + 1, loop, 0)
+    steps = pl.cdiv(groups + 2, UNROLL)
+    lax.fori_loop(0, steps, loop, 0)
+    for m in range(MXUS):
+        pltpu.matmul_acc_lhs(accs[m][0], first_w[:CHUNK], 0)
+        pltpu.matmul_pop(accs[m][0])
     for s in range(slots):
 
         @pl.when((metas[s][0] >= 0) & (starts[s] // batch > steps))
@@ -209,23 +258,12 @@
         block_col = jnp.maximum(metas[s][2], 0)
         row_ok = valid_row(resolved_ref, lengths_ref, member, block_row, side)
         col_ok = valid_row(resolved_ref, lengths_ref, member, block_col, side)
-        keep_row = lax.broadcasted_iota(jnp.int32, (8, side), 0) == 0
-        outer = lax.dot_general(
-            jnp.where(keep_row, row_ok, 0.0),
-            jnp.where(keep_row, col_ok, 0.0),
-            (((0,), (0,)), ((), ())),
-            preferred_element_type=F32,
-        )
-        mass = sums[pl.ds(s * side, side), 0, :]
-        inverse = 1.0 / mass
-        expected = sums[pl.ds(s * side, side), 1, :] * inverse
-        high = sums[pl.ds(s * side, side), 2 + 2 * s, :]
-        low = sums[pl.ds(s * side, side), 3 + 2 * s, :]
-        errors[s] = jnp.where(outer > 0, expected, 0.0)
-        term = jnp.where(outer > 0, (high + low) * inverse, 0.0)
-        tm_sums[s] = lax.dot_general(
-            jnp.ones((PAD, side), F32), term, NT, preferred_element_type=F32, precision=HIGHEST
-        )
+        outer = jnp.transpose(jnp.broadcast_to(row_ok, (side, side))) * col_ok
+        rows = pl.ds(s * side, side)
+        errors[s] = jnp.where(outer > 0, found_error[rows], 0.0)
+        term = jnp.where(outer > 0, found_term[rows], 0.0)
+        tm_row = jnp.sum(jnp.transpose(term), axis=0, keepdims=True)
+        tm_sums[s] = jnp.broadcast_to(tm_row, (PAD, side))
 
     for shift in range(n_cplx):
         owner = lax.rem(cplx_index + shift, n_cplx)
@@ -239,6 +277,13 @@
             first = pl.multiple_of(part * rows_each, rows_each)
             out[:rows_each] = errors[chosen, pl.ds(first, rows_each)]
             out[rows_each:] = tm_sums[chosen]
+
+
+def head_kernel(dims, *refs):
+    _, _, _, _, _, width, hid, bins, _ = dims
+    chunks = (hid + bins + width) // CHUNK
+    accs = [pltpu.ACC(m)((CHUNK, 2 * width), F32) for _ in range(chunks + 1) for m in range(MXUS)]
+    pl.run_scoped(functools.partial(head_body, dims, *refs), *accs)
 
 
 def place_kernel(dims, map_ref, *rest):
@@ -342,7 +387,6 @@
     smem = pl.BlockSpec(memory_space=pltpu.SMEM)
     vmem = pl.BlockSpec(memory_space=pltpu.VMEM)
     axes = ("tile", "cplx")
-    sum_count = -(-(2 + 2 * slots) // 8) * 8
     lanes = GROUP * side
 
     def move(value, block_shift, part_shift, cplx_shift):
@@ -368,20 +412,22 @@
             pltpu.VMEM((hid + bins + width, 2 * width), BF16),
             pltpu.VMEM((bins, hid), BF16),
             pltpu.VMEM((bins, 128), F32),
-            pltpu.VMEM((sum_count, bins), BF16),
+            pltpu.VMEM((bins, 128), F32),
+            pltpu.VMEM((slots + 1, bins, 128), F32),
             pltpu.VMEM((2, hid, lanes), BF16),
             pltpu.VMEM((2, bins, lanes), F32),
             pltpu.VMEM((2, 8, lanes), F32),
             pltpu.VMEM((2, bins, lanes), F32),
-            pltpu.VMEM((slots * side + 8, sum_count, side), F32),
+            pltpu.VMEM((slots * side + 8, side), F32),
+            pltpu.VMEM((slots * side + 8, side), F32),
             pltpu.VMEM((slots, side, side), F32),
             pltpu.VMEM((slots, PAD, side), F32),
-            pltpu.SMEM((slots * side + 64,), jnp.int32),
+            pltpu.SMEM((slots * side + GROUP * (UNROLL + 4),), jnp.int32),
             pltpu.SemaphoreType.DMA((slots,)),
         ],
         compiler_params=pltpu.CompilerParams(vmem_limit_bytes=VMEM_LIMIT),
     )(
-        tile_map,
+        tile_map.T,
         lengths,
         resolved,
         resolved,
@@ -389,7 +435,7 @@
         ln_gain.reshape(1, width),
         w_in,
         w_out,
-        w_head,
+        w_head.T,
         head_bias.reshape(1, bins),
     )
     moved = []
@@ -408,7 +454,8 @@
         in_specs=[smem] + [vmem] * len(moved),
         out_specs=[vmem] * blocks,
         scratch_shapes=[pltpu.VMEM((tm_pad, side), F32)],
-    )(tile_map, *moved)
+        compiler_params=pltpu.CompilerParams(vmem_limit_bytes=VMEM_LIMIT),
+    )(tile_map.T, *moved)
     arrived = [move(shares[b], b, 0, 0) if b else shares[b] for b in range(blocks)]
 
     return pl.pallas_call(
@@ -420,6 +467,7 @@
         ],
         in_specs=[smem, vmem] + [vmem] * blocks,
         out_specs=[vmem, vmem, smem],
+        compiler_params=pltpu.CompilerParams(vmem_limit_bytes=VMEM_LIMIT),
     )(lengths, resolved, *arrived)
 
 

time: 77.5 us -> 62.2 us (0.80)
  local copies, waits for them, and re-layouts: 7.93 us -> 0 us
  Pallas kernels: 32.5 us -> 27 us
  waiting for transfers between devices: 15.2 us -> 13.8 us
  starting transfers between devices: 21 us -> 20 us
    unnamed x38 -> x0, local copies, waits for them, and re-layouts: 7.93 us -> none
    pallas_call x1, Pallas kernels: 27.8 us -> 23 us  [shards(): pl.pallas_call(functools.partial(head_kernel, (n_cplx, parts, cpx_dev, sl...]
    ppermute x10, waiting for transfers between devices: 15.2 us -> 13.8 us  [move(): return lax.ppermute(value, axes, pairs)]
    ppermute x10, starting transfers between devices: 21 us -> 20 us  [move(): return lax.ppermute(value, axes, pairs)]
  transfers between devices with their start and end apart: 10 -> 10, of which waited for: 6 -> 5; matrix products, arithmetic and copies ran while one was open for 0% -> 0% of each run, Pallas kernels for 0% -> 0%
where the time goes in v2:
time: 62.2 us; the launch traced here: 61.4 us
  Pallas kernels  27 us (43%)
  starting transfers between devices  20 us (32%)
  waiting for transfers between devices  13.8 us (22%)
  between operations  0.66 us (1%)
    pallas_call x1, Pallas kernels, shards(): pl.pallas_call(functools.partial(head_kernel, (n_cplx, parts, cpx_dev, sl...  23 us
    ppermute x10, starting transfers between devices, move(): return lax.ppermute(value, axes, pairs)  20 us
    ppermute x10, waiting for transfers between devices, move(): return lax.ppermute(value, axes, pairs)  13.8 us
    pallas_call x1, Pallas kernels, shards(): pl.pallas_call(functools.partial(place_kernel, (n_cplx, parts, cpx_dev, s...  2.13 us
    pallas_call x1, Pallas kernels, shards(): pl.pallas_call(functools.partial(finish_kernel, (parts, cpx_dev, blocks,...  1.88 us
  transfers between devices with their start and end apart: 10, of which 5 were waited for; matrix products, arithmetic and copies ran while one was open for 0% of the time, Pallas kernels for 0%

profile of v2, /device:TPU:9, one launch (start us, length us, event | category | flops | bytes accessed | tf_op | source)
XLA Modules:
  0.0 61.4 jit_solution(11600760542701524339)
XLA Ops:
  0.6 23.0 %shard_map.112 = (f32[72,128]{1,0:T(8,128)}, f32[72,128]{1,0:T(8,128)}, f32[72,128]{1,0:T(8,128)}, f32[72,128]{1,0:T(8,128)}, f32[72,128]{1,0:T(8,128)}, /*index...) custom-call(s32[3,96]{1,0:T(4,128)} %bitcast.5, s32[4]{0:T(128)} %lengths_ref.1, s32[4,512]{1,0:T(4,128)} %resolved_ref.1, ...), custom_call_target="tpu_custom_call" | custom-call | tf_op jit(solution)/shard_map/pallas_call | solution.py:403
  23.6 0.1 collective-permute-start
  23.7 1.9 %collective-permute-start.1 = (f32[72,128]{1,0:T(8,128)}, f32[72,128]{1,0:T(8,128)}, u32[]{:S(2)}, u32[]{:S(2)}) collective-permute-start(f32[72,128]{1,0:T(8,128)} %get-tuple-element.17), channel_id=1, source_target_pairs={{0,1},{1,2},{2,3},{3,0},{4,5},{5,6},{6,7},{7,4},{8,9},{9,10},{10,1... | collective-permute-start | bytes 110600 | tf_op jit(solution)/shard_map/ppermute | solution.py:400
  25.5 1.4 %collective-permute-start.2 = (f32[72,128]{1,0:T(8,128)}, f32[72,128]{1,0:T(8,128)}, u32[]{:S(2)}, u32[]{:S(2)}) collective-permute-start(f32[72,128]{1,0:T(8,128)} %get-tuple-element.18), channel_id=1, source_target_pairs={{0,5},{1,6},{2,7},{3,4},{4,1},{5,2},{6,3},{7,0},{8,13},{9,14},{10,... | collective-permute-start | bytes 110600 | tf_op jit(solution)/shard_map/ppermute | solution.py:400
  26.9 0.2 collective-permute-start.3
  27.2 1.2 %collective-permute-start.4 = (f32[72,128]{1,0:T(8,128)}, f32[72,128]{1,0:T(8,128)}, u32[]{:S(2)}, u32[]{:S(2)}) collective-permute-start(f32[72,128]{1,0:T(8,128)} %get-tuple-element.20), channel_id=1, source_target_pairs={{0,6},{1,7},{2,4},{3,5},{4,2},{5,3},{6,0},{7,1},{8,14},{9,15},{10,... | collective-permute-start | bytes 110600 | tf_op jit(solution)/shard_map/ppermute | solution.py:400
  28.4 0.0 collective-permute-done.rest_1_
  28.4 0.7 %collective-permute-start.5 = (f32[72,128]{1,0:T(8,128)}, f32[72,128]{1,0:T(8,128)}, u32[]{:S(2)}, u32[]{:S(2)}) collective-permute-start(f32[72,128]{1,0:T(8,128)} %get-tuple-element.21), channel_id=1, source_target_pairs={{0,3},{1,0},{2,1},{3,2},{4,7},{5,4},{6,5},{7,6},{8,11},{9,8},{10,9... | collective-permute-start | bytes 110600 | tf_op jit(solution)/shard_map/ppermute | solution.py:400
  29.2 0.0 collective-permute-done.1.rest_2_
  29.2 1.6 %collective-permute-start.6 = (f32[72,128]{1,0:T(8,128)}, f32[72,128]{1,0:T(8,128)}, u32[]{:S(2)}, u32[]{:S(2)}) collective-permute-start(f32[72,128]{1,0:T(8,128)} %get-tuple-element.22), channel_id=1, source_target_pairs={{0,7},{1,4},{2,5},{3,6},{4,3},{5,0},{6,1},{7,2},{8,15},{9,12},{10,... | collective-permute-start | bytes 110600 | tf_op jit(solution)/shard_map/ppermute | solution.py:400
  30.8 0.0 collective-permute-done.2.rest_3_
  30.8 0.0 collective-permute-done.3.rest_4_
  30.8 0.4 collective-permute-done.4.rest_5_
  31.2 1.2 %collective-permute-done.5.rest_6_ = f32[72,128]{1,0:T(8,128)} collective-permute-done((f32[72,128]{1,0:T(8,128)}, f32[72,128]{1,0:T(8,128)}, u32[]{:S(2)}, u32[]{:S(2)}) %collective-permute-start.5) | collective-permute-done | bytes 36896 | tf_op jit(solution)/shard_map/ppermute | solution.py:400
  32.4 1.3 %collective-permute-done.6.rest_7_ = f32[72,128]{1,0:T(8,128)} collective-permute-done((f32[72,128]{1,0:T(8,128)}, f32[72,128]{1,0:T(8,128)}, u32[]{:S(2)}, u32[]{:S(2)}) %collective-permute-start.6) | collective-permute-done | bytes 36896 | tf_op jit(solution)/shard_map/ppermute | solution.py:400
  33.8 2.1 %shard_map.113 = (f32[264,128]{1,0:T(8,128)}, f32[264,128]{1,0:T(8,128)}, f32[264,128]{1,0:T(8,128)}, f32[264,128]{1,0:T(8,128)}) custom-call(s32[3,96]{1,0:T(4,128)} %bitcast.6, f32[72,128]{1,0:T(8,128)} %get-tuple-element.15.rest_0_, f32[72,128]{1,0:T(8,128)} %collective-permute-done.rest_1_, f32[72,128]{1,0:T(8,128)} %collective-permute-done.1.rest_2_, ...), custom_call_target="tpu_custom_call" | custom-call | tf_op jit(solution)/shard_map/pallas_call | solution.py:449
  35.9 11.6 %collective-permute-start.7 = (f32[264,128]{1,0:T(8,128)}, f32[264,128]{1,0:T(8,128)}, u32[]{:S(2)}, u32[]{:S(2)}) collective-permute-start(f32[264,128]{1,0:T(8,128)} %get-tuple-element.24), channel_id=1, source_target_pairs={{0,8},{1,9},{2,10},{3,11},{4,12},{5,13},{6,14},{7,15},{8,16},{9,17... | collective-permute-start | bytes 405512 | tf_op jit(solution)/shard_map/ppermute | solution.py:400
  47.5 0.0 collective-permute-start.8
  47.5 1.2 %collective-permute-start.9 = (f32[264,128]{1,0:T(8,128)}, f32[264,128]{1,0:T(8,128)}, u32[]{:S(2)}, u32[]{:S(2)}) collective-permute-start(f32[264,128]{1,0:T(8,128)} %get-tuple-element.26), channel_id=1, source_target_pairs={{0,24},{1,25},{2,26},{3,27},{4,28},{5,29},{6,30},{7,31},{8,0},{9,1... | collective-permute-start | bytes 405512 | tf_op jit(solution)/shard_map/ppermute | solution.py:400
  48.7 8.3 %collective-permute-done.7.rest_1_ = f32[264,128]{1,0:T(8,128)} collective-permute-done((f32[264,128]{1,0:T(8,128)}, f32[264,128]{1,0:T(8,128)}, u32[]{:S(2)}, u32[]{:S(2)}) %collective-permute-start.7) | collective-permute-done | bytes 135200 | tf_op jit(solution)/shard_map/ppermute | solution.py:400
  57.0 2.5 %collective-permute-done.8.rest_2_ = f32[264,128]{1,0:T(8,128)} collective-permute-done((f32[264,128]{1,0:T(8,128)}, f32[264,128]{1,0:T(8,128)}, u32[]{:S(2)}, u32[]{:S(2)}) %collective-permute-start.8) | collective-permute-done | bytes 135200 | tf_op jit(solution)/shard_map/ppermute | solution.py:400
  59.5 0.0 collective-permute-done.9.rest_3_
  59.5 1.9 %shard_map.114 = (f32[1,64,512]{2,1,0:T(8,128)}, f32[1,64]{1,0:T(1,128)}, f32[1]{0:T(128)}) custom-call(s32[4]{0:T(128)} %lengths_ref.1, s32[4,512]{1,0:T(4,128)} %resolved_ref.1, f32[264,128]{1,0:T(8,128)} %get-tuple-element.23.rest_0_, f32[264,128]{1,0:T(8,128)} %collective-permute-done.7.rest_1_, f32[264,128]{1,0:T(8,128)} %collective-permute-done.8.rest_2_, ...), custom_call_target="tpu_custom_call" | custom-call | tf_op jit(solution)/shard_map/pallas_call | solution.py:461
Async XLA Ops:
  23.6 4.8 %collective-permute-start = (f32[72,128]{1,0:T(8,128)}, f32[72,128]{1,0:T(8,128)}, u32[]{:S(2)}, u32[]{:S(2)}) collective-permute-start(f32[72,128]{1,0:T(8,128)} %get-tuple-element.16), channel_id=1, source_target_pairs={{0,4},{1,5},{2,6},{3,7},{4,0},{5,1},{6,2},{7,3},{8,12},{9,13},{10,... | collective-permute-start | bytes 110600 | tf_op jit(solution)/shard_map/ppermute | solution.py:400
  23.7 5.5 %collective-permute-start.1 = (f32[72,128]{1,0:T(8,128)}, f32[72,128]{1,0:T(8,128)}, u32[]{:S(2)}, u32[]{:S(2)}) collective-permute-start(f32[72,128]{1,0:T(8,128)} %get-tuple-element.17), channel_id=1, source_target_pairs={{0,1},{1,2},{2,3},{3,0},{4,5},{5,6},{6,7},{7,4},{8,9},{9,10},{10,1... | collective-permute-start | bytes 110600 | tf_op jit(solution)/shard_map/ppermute | solution.py:400
  25.5 5.2 %collective-permute-start.2 = (f32[72,128]{1,0:T(8,128)}, f32[72,128]{1,0:T(8,128)}, u32[]{:S(2)}, u32[]{:S(2)}) collective-permute-start(f32[72,128]{1,0:T(8,128)} %get-tuple-element.18), channel_id=1, source_target_pairs={{0,5},{1,6},{2,7},{3,4},{4,1},{5,2},{6,3},{7,0},{8,13},{9,14},{10,... | collective-permute-start | bytes 110600 | tf_op jit(solution)/shard_map/ppermute | solution.py:400
  26.9 3.8 %collective-permute-start.3 = (f32[72,128]{1,0:T(8,128)}, f32[72,128]{1,0:T(8,128)}, u32[]{:S(2)}, u32[]{:S(2)}) collective-permute-start(f32[72,128]{1,0:T(8,128)} %get-tuple-element.19), channel_id=1, source_target_pairs={{0,2},{1,3},{2,0},{3,1},{4,6},{5,7},{6,4},{7,5},{8,10},{9,11},{10,... | collective-permute-start | bytes 110600 | tf_op jit(solution)/shard_map/ppermute | solution.py:400
  27.2 4.0 %collective-permute-start.4 = (f32[72,128]{1,0:T(8,128)}, f32[72,128]{1,0:T(8,128)}, u32[]{:S(2)}, u32[]{:S(2)}) collective-permute-start(f32[72,128]{1,0:T(8,128)} %get-tuple-element.20), channel_id=1, source_target_pairs={{0,6},{1,7},{2,4},{3,5},{4,2},{5,3},{6,0},{7,1},{8,14},{9,15},{10,... | collective-permute-start | bytes 110600 | tf_op jit(solution)/shard_map/ppermute | solution.py:400
  28.4 4.0 %collective-permute-start.5 = (f32[72,128]{1,0:T(8,128)}, f32[72,128]{1,0:T(8,128)}, u32[]{:S(2)}, u32[]{:S(2)}) collective-permute-start(f32[72,128]{1,0:T(8,128)} %get-tuple-element.21), channel_id=1, source_target_pairs={{0,3},{1,0},{2,1},{3,2},{4,7},{5,4},{6,5},{7,6},{8,11},{9,8},{10,9... | collective-permute-start | bytes 110600 | tf_op jit(solution)/shard_map/ppermute | solution.py:400
  29.2 4.6 %collective-permute-start.6 = (f32[72,128]{1,0:T(8,128)}, f32[72,128]{1,0:T(8,128)}, u32[]{:S(2)}, u32[]{:S(2)}) collective-permute-start(f32[72,128]{1,0:T(8,128)} %get-tuple-element.22), channel_id=1, source_target_pairs={{0,7},{1,4},{2,5},{3,6},{4,3},{5,0},{6,1},{7,2},{8,15},{9,12},{10,... | collective-permute-start | bytes 110600 | tf_op jit(solution)/shard_map/ppermute | solution.py:400
  35.9 21.1 %collective-permute-start.7 = (f32[264,128]{1,0:T(8,128)}, f32[264,128]{1,0:T(8,128)}, u32[]{:S(2)}, u32[]{:S(2)}) collective-permute-start(f32[264,128]{1,0:T(8,128)} %get-tuple-element.24), channel_id=1, source_target_pairs={{0,8},{1,9},{2,10},{3,11},{4,12},{5,13},{6,14},{7,15},{8,16},{9,17... | collective-permute-start | bytes 405512 | tf_op jit(solution)/shard_map/ppermute | solution.py:400
  47.5 12.0 %collective-permute-start.8 = (f32[264,128]{1,0:T(8,128)}, f32[264,128]{1,0:T(8,128)}, u32[]{:S(2)}, u32[]{:S(2)}) collective-permute-start(f32[264,128]{1,0:T(8,128)} %get-tuple-element.25), channel_id=1, source_target_pairs={{0,16},{1,17},{2,18},{3,19},{4,20},{5,21},{6,22},{7,23},{8,24},{9,... | collective-permute-start | bytes 405512 | tf_op jit(solution)/shard_map/ppermute | solution.py:400
  47.5 12.0 %collective-permute-start.9 = (f32[264,128]{1,0:T(8,128)}, f32[264,128]{1,0:T(8,128)}, u32[]{:S(2)}, u32[]{:S(2)}) collective-permute-start(f32[264,128]{1,0:T(8,128)} %get-tuple-element.26), channel_id=1, source_target_pairs={{0,24},{1,25},{2,26},{3,27},{4,28},{5,29},{6,30},{7,31},{8,0},{9,1... | collective-permute-start | bytes 405512 | tf_op jit(solution)/shard_map/ppermute | solution.py:400

commit v3 on v2

--- a/solution.py
+++ b/solution.py
@@ -46,21 +46,22 @@
 
 def head_body(
     dims,
-    map_ref,
-    lengths_ref,
-    flags_ref,
-    resolved_ref,
     tiles_ref,
-    gain_ref,
-    w_in_ref,
-    w_out_ref,
-    w_head_ref,
-    bias_ref,
     *rest,
 ):
     n_cplx, parts, cpx_dev, slots, side, width, hid, bins, rows_each = dims
+    operands, rest = rest[:8], rest[8:]
     outs = rest[: n_cplx * parts]
     (
+        map_ref,
+        lengths_ref,
+        resolved_ref,
+        gain_ref,
+        w_in_ref,
+        w_out_ref,
+        w_head_ref,
+        bias_ref,
+        operand_sems,
         tiles,
         first_w,
         second_w,
@@ -83,7 +84,6 @@
     tile_index = lax.axis_index("tile")
     cplx_index = lax.axis_index("cplx")
     part_index = lax.rem(tile_index, parts)
-    metas = own_slots(map_ref, (tile_index * n_cplx + cplx_index) * slots, slots)
     total = slots * side
 
     def slot_copy(s):
@@ -91,35 +91,48 @@
             tiles_ref.at[s], tiles.at[pl.ds(s * side, side)], sems.at[s]
         )
 
+    places = (
+        map_ref, lengths_ref, resolved_ref, gain_ref, w_in_ref, w_out_ref, w_head_ref, bias_ref
+    )
+    loads = [
+        pltpu.make_async_copy(source, place, operand_sems.at[n])
+        for n, (source, place) in enumerate(zip(operands, places))
+    ]
+    for load in loads[:3]:
+        load.start()
+    slot_copy(0).start()
+    for load in loads[3:]:
+        load.start()
+    for load in loads[:3]:
+        load.wait()
+    metas = own_slots(map_ref, (tile_index * n_cplx + cplx_index) * slots, slots)
+
+    lane = lax.broadcasted_iota(jnp.int32, (1, side), 1)
+    power = (1 << (lane & 15)).astype(F32)
+    masks = []
     for s in range(slots):
-
-        @pl.when(metas[s][0] >= 0)
-        def _(s=s):
-            slot_copy(s).start()
-
+        member = jnp.maximum(metas[s][0], 0)
+        found = valid_row(resolved_ref, lengths_ref, member, jnp.maximum(metas[s][1], 0), side)
+        found = jnp.where(metas[s][0] >= 0, found * power, 0.0)
+        masks.append(
+            [
+                jnp.sum(jnp.where(lane // 16 == g, found, 0.0)).astype(jnp.int32)
+                for g in range(side // 16)
+            ]
+        )
     count = jnp.int32(0)
     starts = []
-    unroll = 8
     for s in range(slots):
         starts.append(count)
-        member = jnp.maximum(metas[s][0], 0)
-        base = jnp.maximum(metas[s][1], 0) * side
-        limit = jnp.where(metas[s][0] >= 0, jnp.minimum(lengths_ref[member] - base, side), 0)
-        limit = jnp.maximum(limit, 0)
-
-        def step(g, cnt, s=s, member=member, base=base, limit=limit):
-            for u in range(unroll):
-                row = g * unroll + u
-                order[cnt] = s * side + row
-                keep = (flags_ref[member, base + row] > 0) & (row < limit)
-                cnt = cnt + keep.astype(jnp.int32)
-            return cnt
-
-        count = lax.fori_loop(0, pl.cdiv(limit, unroll), step, count)
+        for row in range(side):
+            order[count] = s * side + row
+            count = count + ((masks[s][row // 16] >> (row % 16)) & 1)
     batch = UNROLL * GROUP
     for u in range(4 * GROUP + batch):
         order[count + u] = total
 
+    for load in loads[3:]:
+        load.wait()
     w_in_t = jnp.transpose(w_in_ref[...].astype(F32)) * gain_ref[...]
     w_in_t = w_in_t - jnp.mean(w_in_t, axis=1, keepdims=True)
     head_t = w_head_ref[...].astype(F32)
@@ -164,6 +177,14 @@
             pairs = jnp.concatenate([pairs, pairs], axis=1)
             pltpu.matmul_push_rhs(pairs, 0, m, transpose=True)
 
+    def measure(first_row, u, slot):
+        values = jnp.transpose(tiles[order[first_row + u]]).astype(F32)
+        centred = values - jnp.sum(values, axis=0, keepdims=True) * (1.0 / width)
+        variance = jnp.sum(centred * centred, axis=0, keepdims=True) * (1.0 / width)
+        spread[slot, :, u * side : (u + 1) * side] = jnp.broadcast_to(
+            lax.rsqrt(variance + EPS), (8, side)
+        )
+
     def take(slot, chunk, m, variance):
         value = pltpu.matmul_pop(accs[m][chunk])
         at = chunk * CHUNK
@@ -189,21 +210,24 @@
             found_error[pl.ds(row, 1)] = expected * inverse
             found_term[pl.ds(row, 1)] = term * inverse
 
-    def stage(group, slot):
+    def stage(group, slot, direct_spread):
         other = 1 - slot
         variance = [None] * MXUS
-        for chunk in range(chunks):
+        used = (hid + bins) // CHUNK if direct_spread else chunks
+        for chunk in range(used):
             for m in range(MXUS):
                 left = first_w[chunk * CHUNK : (chunk + 1) * CHUNK]
                 pltpu.matmul_acc_lhs(accs[m][chunk], left, 0 if chunk == 0 else None)
-            if chunk == 1 or chunk == 4:
-                k = chunk // 4
+            if chunk == 2 or chunk == 6:
+                k = chunk // 6
                 for m in range(MXUS):
                     right = hidden[other, k * depth : (k + 1) * depth, m * half : (m + 1) * half]
                     pltpu.matmul_push_rhs(right, k, m)
             if chunk >= 1:
                 for m in range(MXUS):
                     take(slot, chunk - 1, m, variance)
+            if direct_spread and chunk % 2 == 0 and chunk // 2 < GROUP:
+                measure(group * GROUP, chunk // 2, slot)
         for k in range(hid // depth):
             for m in range(MXUS):
                 pltpu.matmul_acc_lhs(accs[m][chunks], second_w[:, k * depth : (k + 1) * depth], k)
@@ -211,12 +235,11 @@
                 push_pairs((group + 1) * GROUP)
         weigh((group - 2) * GROUP, slot)
         for m in range(MXUS):
-            take(slot, chunks - 1, m, variance)
-            spread_now = jnp.sum(variance[m], axis=0, keepdims=True) * (1.0 / width)
-            spread[slot, :, m * half : (m + 1) * half] = jnp.broadcast_to(
-                lax.rsqrt(spread_now + EPS), (8, half)
-            )
+            take(slot, used - 1, m, variance)
             cols = slice(m * half, (m + 1) * half)
+            if not direct_spread:
+                spread_now = jnp.sum(variance[m], axis=0, keepdims=True) * (1.0 / width)
+                spread[slot, :, cols] = jnp.broadcast_to(lax.rsqrt(spread_now + EPS), (8, half))
             scale = spread[other, :1, cols]
             change = pltpu.matmul_pop(accs[m][chunks])
             bias = jnp.concatenate([bias_tile[...]] * (half // 128), axis=1)
@@ -226,19 +249,22 @@
     groups = pl.cdiv(count, GROUP)
 
     def wait_for(g):
-        for s in range(slots):
-
-            @pl.when((metas[s][0] >= 0) & (starts[s] // batch == g))
+        for s in range(1, slots):
+
+            @pl.when(starts[s] // batch == g)
             def _(s=s):
                 slot_copy(s).wait()
 
+    slot_copy(0).wait()
+    for s in range(1, slots):
+        slot_copy(s).start()
     wait_for(0)
     push_pairs(0)
 
     def loop(g, carry):
         wait_for(g + 1)
         for u in range(UNROLL):
-            stage(g * UNROLL + u, u % 2)
+            stage(g * UNROLL + u, u % 2, True)
         return carry
 
     steps = pl.cdiv(groups + 2, UNROLL)
@@ -246,9 +272,9 @@
     for m in range(MXUS):
         pltpu.matmul_acc_lhs(accs[m][0], first_w[:CHUNK], 0)
         pltpu.matmul_pop(accs[m][0])
-    for s in range(slots):
-
-        @pl.when((metas[s][0] >= 0) & (starts[s] // batch > steps))
+    for s in range(1, slots):
+
+        @pl.when(starts[s] // batch > steps)
         def _(s=s):
             slot_copy(s).wait()
 
@@ -405,9 +431,18 @@
             head_kernel, (n_cplx, parts, cpx_dev, slots, side, width, hid, bins, rows_each)
         ),
         out_shape=[piece] * (n_cplx * parts),
-        in_specs=[smem, smem, smem, vmem, pl.BlockSpec(memory_space=pl.ANY)] + [vmem] * 5,
+        in_specs=[pl.BlockSpec(memory_space=pl.ANY)] * 9,
         out_specs=[vmem] * (n_cplx * parts),
         scratch_shapes=[
+            pltpu.SMEM(tile_map.shape[::-1], jnp.int32),
+            pltpu.SMEM(lengths.shape, jnp.int32),
+            pltpu.VMEM(resolved.shape, jnp.int32),
+            pltpu.VMEM((1, width), F32),
+            pltpu.VMEM(w_in.shape, BF16),
+            pltpu.VMEM(w_out.shape, BF16),
+            pltpu.VMEM(w_head.shape[::-1], BF16),
+            pltpu.VMEM((1, bins), F32),
+            pltpu.SemaphoreType.DMA((8,)),
             pltpu.VMEM((slots * side + 8, side, width), BF16),
             pltpu.VMEM((hid + bins + width, 2 * width), BF16),
             pltpu.VMEM((bins, hid), BF16),
@@ -427,11 +462,10 @@
         ],
         compiler_params=pltpu.CompilerParams(vmem_limit_bytes=VMEM_LIMIT),
     )(
+        pair_tiles,
         tile_map.T,
         lengths,
         resolved,
-        resolved,
-        pair_tiles,
         ln_gain.reshape(1, width),
         w_in,
         w_out,

time: 62.2 us -> 59 us (0.949); the launches traced: 61.4 us -> 59.3 us
  starting transfers between devices: 20 us -> 17.7 us
  waiting for transfers between devices: 13.8 us -> 15.7 us
  Pallas kernels: 27 us -> 25.2 us
    ppermute x10, starting transfers between devices: 20 us -> 17.7 us  [move(): return lax.ppermute(value, axes, pairs)]
    ppermute x10, waiting for transfers between devices: 13.8 us -> 15.7 us  [move(): return lax.ppermute(value, axes, pairs)]
    pallas_call x1, Pallas kernels: 23 us -> 21.2 us  [shards(): pl.pallas_call(functools.partial(head_kernel, (n_cplx, parts, cpx_dev, sl...]
  transfers between devices with their start and end apart: 10 -> 10, of which waited for: 5 -> 7; matrix products, arithmetic and copies ran while one was open for 0% -> 0% of each run, Pallas kernels for 0% -> 0%
where the time goes in v3:
time: 59 us; the launch traced here: 59.3 us
  Pallas kernels  25.2 us (43%)
  starting transfers between devices  17.7 us (30%)
  waiting for transfers between devices  15.7 us (27%)
  between operations  0.66 us (1%)
    pallas_call x1, Pallas kernels, shards(): pl.pallas_call(functools.partial(head_kernel, (n_cplx, parts, cpx_dev, sl...  21.2 us
    ppermute x10, starting transfers between devices, move(): return lax.ppermute(value, axes, pairs)  17.7 us
    ppermute x10, waiting for transfers between devices, move(): return lax.ppermute(value, axes, pairs)  15.7 us
    pallas_call x1, Pallas kernels, shards(): pl.pallas_call(functools.partial(place_kernel, (n_cplx, parts, cpx_dev, s...  2.13 us
    pallas_call x1, Pallas kernels, shards(): pl.pallas_call(functools.partial(finish_kernel, (parts, cpx_dev, blocks,...  1.88 us
  transfers between devices with their start and end apart: 10, of which 7 were waited for; matrix products, arithmetic and copies ran while one was open for 0% of the time, Pallas kernels for 0%

profile of v3, /device:TPU:9, one launch (start us, length us, event | category | flops | bytes accessed | tf_op | source)
XLA Modules:
  0.0 59.3 jit_solution(237007951123111406)
XLA Ops:
  0.6 21.2 %shard_map.112 = (f32[72,128]{1,0:T(8,128)}, f32[72,128]{1,0:T(8,128)}, f32[72,128]{1,0:T(8,128)}, f32[72,128]{1,0:T(8,128)}, f32[72,128]{1,0:T(8,128)}, /*index...) custom-call(bf16[3,128,128,128]{3,2,1,0:T(8,128)(2,1)} %refs_0_.1, s32[3,96]{1,0:T(4,128)} %bitcast.5, ...), custom_call_target="tpu_custom_call" | custom-call | tf_op jit(solution)/shard_map/pallas_call | solution.py:429
  21.8 0.1 collective-permute-start
  21.9 11.5 %collective-permute-start.1 = (f32[72,128]{1,0:T(8,128)}, f32[72,128]{1,0:T(8,128)}, u32[]{:S(2)}, u32[]{:S(2)}) collective-permute-start(f32[72,128]{1,0:T(8,128)} %get-tuple-element.17), channel_id=1, source_target_pairs={{0,1},{1,2},{2,3},{3,0},{4,5},{5,6},{6,7},{7,4},{8,9},{9,10},{10,1... | collective-permute-start | bytes 110600 | tf_op jit(solution)/shard_map/ppermute | solution.py:426
  33.4 0.0 collective-permute-start.2
  33.4 0.2 collective-permute-start.3
  33.6 2.2 %collective-permute-start.4 = (f32[72,128]{1,0:T(8,128)}, f32[72,128]{1,0:T(8,128)}, u32[]{:S(2)}, u32[]{:S(2)}) collective-permute-start(f32[72,128]{1,0:T(8,128)} %get-tuple-element.20), channel_id=1, source_target_pairs={{0,6},{1,7},{2,4},{3,5},{4,2},{5,3},{6,0},{7,1},{8,14},{9,15},{10,... | collective-permute-start | bytes 110600 | tf_op jit(solution)/shard_map/ppermute | solution.py:426
  35.8 0.0 collective-permute-done.rest_1_
  35.8 1.2 %collective-permute-start.5 = (f32[72,128]{1,0:T(8,128)}, f32[72,128]{1,0:T(8,128)}, u32[]{:S(2)}, u32[]{:S(2)}) collective-permute-start(f32[72,128]{1,0:T(8,128)} %get-tuple-element.21), channel_id=1, source_target_pairs={{0,3},{1,0},{2,1},{3,2},{4,7},{5,4},{6,5},{7,6},{8,11},{9,8},{10,9... | collective-permute-start | bytes 110600 | tf_op jit(solution)/shard_map/ppermute | solution.py:426
  37.0 0.0 collective-permute-done.1.rest_2_
  37.0 0.0 collective-permute-start.6
  37.0 0.4 collective-permute-done.2.rest_3_
  37.4 0.0 collective-permute-done.3.rest_4_
  37.4 0.4 collective-permute-done.4.rest_5_
  37.8 1.6 %collective-permute-done.5.rest_6_ = f32[72,128]{1,0:T(8,128)} collective-permute-done((f32[72,128]{1,0:T(8,128)}, f32[72,128]{1,0:T(8,128)}, u32[]{:S(2)}, u32[]{:S(2)}) %collective-permute-start.5) | collective-permute-done | bytes 36896 | tf_op jit(solution)/shard_map/ppermute | solution.py:426
  39.5 2.1 %collective-permute-done.6.rest_7_ = f32[72,128]{1,0:T(8,128)} collective-permute-done((f32[72,128]{1,0:T(8,128)}, f32[72,128]{1,0:T(8,128)}, u32[]{:S(2)}, u32[]{:S(2)}) %collective-permute-start.6) | collective-permute-done | bytes 36896 | tf_op jit(solution)/shard_map/ppermute | solution.py:426
  41.6 2.1 %shard_map.113 = (f32[264,128]{1,0:T(8,128)}, f32[264,128]{1,0:T(8,128)}, f32[264,128]{1,0:T(8,128)}, f32[264,128]{1,0:T(8,128)}) custom-call(s32[3,96]{1,0:T(4,128)} %bitcast.6, f32[72,128]{1,0:T(8,128)} %get-tuple-element.15.rest_0_, f32[72,128]{1,0:T(8,128)} %collective-permute-done.rest_1_, f32[72,128]{1,0:T(8,128)} %collective-permute-done.1.rest_2_, ...), custom_call_target="tpu_custom_call" | custom-call | tf_op jit(solution)/shard_map/pallas_call | solution.py:483
  43.7 1.3 %collective-permute-start.7 = (f32[264,128]{1,0:T(8,128)}, f32[264,128]{1,0:T(8,128)}, u32[]{:S(2)}, u32[]{:S(2)}) collective-permute-start(f32[264,128]{1,0:T(8,128)} %get-tuple-element.24), channel_id=1, source_target_pairs={{0,8},{1,9},{2,10},{3,11},{4,12},{5,13},{6,14},{7,15},{8,16},{9,17... | collective-permute-start | bytes 405512 | tf_op jit(solution)/shard_map/ppermute | solution.py:426
  45.0 0.0 collective-permute-start.8
  45.0 1.2 %collective-permute-start.9 = (f32[264,128]{1,0:T(8,128)}, f32[264,128]{1,0:T(8,128)}, u32[]{:S(2)}, u32[]{:S(2)}) collective-permute-start(f32[264,128]{1,0:T(8,128)} %get-tuple-element.26), channel_id=1, source_target_pairs={{0,24},{1,25},{2,26},{3,27},{4,28},{5,29},{6,30},{7,31},{8,0},{9,1... | collective-permute-start | bytes 405512 | tf_op jit(solution)/shard_map/ppermute | solution.py:426
  46.3 8.1 %collective-permute-done.7.rest_1_ = f32[264,128]{1,0:T(8,128)} collective-permute-done((f32[264,128]{1,0:T(8,128)}, f32[264,128]{1,0:T(8,128)}, u32[]{:S(2)}, u32[]{:S(2)}) %collective-permute-start.7) | collective-permute-done | bytes 135200 | tf_op jit(solution)/shard_map/ppermute | solution.py:426
  54.4 2.7 %collective-permute-done.8.rest_2_ = f32[264,128]{1,0:T(8,128)} collective-permute-done((f32[264,128]{1,0:T(8,128)}, f32[264,128]{1,0:T(8,128)}, u32[]{:S(2)}, u32[]{:S(2)}) %collective-permute-start.8) | collective-permute-done | bytes 135200 | tf_op jit(solution)/shard_map/ppermute | solution.py:426
  57.0 0.4 collective-permute-done.9.rest_3_
  57.4 1.9 %shard_map.114 = (f32[1,64,512]{2,1,0:T(8,128)}, f32[1,64]{1,0:T(1,128)}, f32[1]{0:T(128)}) custom-call(s32[4]{0:T(128)} %lengths_ref.1, s32[4,512]{1,0:T(4,128)} %resolved_ref.1, f32[264,128]{1,0:T(8,128)} %get-tuple-element.23.rest_0_, f32[264,128]{1,0:T(8,128)} %collective-permute-done.7.rest_1_, f32[264,128]{1,0:T(8,128)} %collective-permute-done.8.rest_2_, ...), custom_call_target="tpu_custom_call" | custom-call | tf_op jit(solution)/shard_map/pallas_call | solution.py:495
Async XLA Ops:
  21.8 13.9 %collective-permute-start = (f32[72,128]{1,0:T(8,128)}, f32[72,128]{1,0:T(8,128)}, u32[]{:S(2)}, u32[]{:S(2)}) collective-permute-start(f32[72,128]{1,0:T(8,128)} %get-tuple-element.16), channel_id=1, source_target_pairs={{0,4},{1,5},{2,6},{3,7},{4,0},{5,1},{6,2},{7,3},{8,12},{9,13},{10,... | collective-permute-start | bytes 110600 | tf_op jit(solution)/shard_map/ppermute | solution.py:426
  21.9 15.1 %collective-permute-start.1 = (f32[72,128]{1,0:T(8,128)}, f32[72,128]{1,0:T(8,128)}, u32[]{:S(2)}, u32[]{:S(2)}) collective-permute-start(f32[72,128]{1,0:T(8,128)} %get-tuple-element.17), channel_id=1, source_target_pairs={{0,1},{1,2},{2,3},{3,0},{4,5},{5,6},{6,7},{7,4},{8,9},{9,10},{10,1... | collective-permute-start | bytes 110600 | tf_op jit(solution)/shard_map/ppermute | solution.py:426
  33.4 4.0 %collective-permute-start.2 = (f32[72,128]{1,0:T(8,128)}, f32[72,128]{1,0:T(8,128)}, u32[]{:S(2)}, u32[]{:S(2)}) collective-permute-start(f32[72,128]{1,0:T(8,128)} %get-tuple-element.18), channel_id=1, source_target_pairs={{0,5},{1,6},{2,7},{3,4},{4,1},{5,2},{6,3},{7,0},{8,13},{9,14},{10,... | collective-permute-start | bytes 110600 | tf_op jit(solution)/shard_map/ppermute | solution.py:426
  33.4 4.0 %collective-permute-start.3 = (f32[72,128]{1,0:T(8,128)}, f32[72,128]{1,0:T(8,128)}, u32[]{:S(2)}, u32[]{:S(2)}) collective-permute-start(f32[72,128]{1,0:T(8,128)} %get-tuple-element.19), channel_id=1, source_target_pairs={{0,2},{1,3},{2,0},{3,1},{4,6},{5,7},{6,4},{7,5},{8,10},{9,11},{10,... | collective-permute-start | bytes 110600 | tf_op jit(solution)/shard_map/ppermute | solution.py:426
  33.6 4.2 %collective-permute-start.4 = (f32[72,128]{1,0:T(8,128)}, f32[72,128]{1,0:T(8,128)}, u32[]{:S(2)}, u32[]{:S(2)}) collective-permute-start(f32[72,128]{1,0:T(8,128)} %get-tuple-element.20), channel_id=1, source_target_pairs={{0,6},{1,7},{2,4},{3,5},{4,2},{5,3},{6,0},{7,1},{8,14},{9,15},{10,... | collective-permute-start | bytes 110600 | tf_op jit(solution)/shard_map/ppermute | solution.py:426
  35.8 3.7 %collective-permute-start.5 = (f32[72,128]{1,0:T(8,128)}, f32[72,128]{1,0:T(8,128)}, u32[]{:S(2)}, u32[]{:S(2)}) collective-permute-start(f32[72,128]{1,0:T(8,128)} %get-tuple-element.21), channel_id=1, source_target_pairs={{0,3},{1,0},{2,1},{3,2},{4,7},{5,4},{6,5},{7,6},{8,11},{9,8},{10,9... | collective-permute-start | bytes 110600 | tf_op jit(solution)/shard_map/ppermute | solution.py:426
  37.0 4.6 %collective-permute-start.6 = (f32[72,128]{1,0:T(8,128)}, f32[72,128]{1,0:T(8,128)}, u32[]{:S(2)}, u32[]{:S(2)}) collective-permute-start(f32[72,128]{1,0:T(8,128)} %get-tuple-element.22), channel_id=1, source_target_pairs={{0,7},{1,4},{2,5},{3,6},{4,3},{5,0},{6,1},{7,2},{8,15},{9,12},{10,... | collective-permute-start | bytes 110600 | tf_op jit(solution)/shard_map/ppermute | solution.py:426
  43.7 10.7 %collective-permute-start.7 = (f32[264,128]{1,0:T(8,128)}, f32[264,128]{1,0:T(8,128)}, u32[]{:S(2)}, u32[]{:S(2)}) collective-permute-start(f32[264,128]{1,0:T(8,128)} %get-tuple-element.24), channel_id=1, source_target_pairs={{0,8},{1,9},{2,10},{3,11},{4,12},{5,13},{6,14},{7,15},{8,16},{9,17... | collective-permute-start | bytes 405512 | tf_op jit(solution)/shard_map/ppermute | solution.py:426
  45.0 12.0 %collective-permute-start.8 = (f32[264,128]{1,0:T(8,128)}, f32[264,128]{1,0:T(8,128)}, u32[]{:S(2)}, u32[]{:S(2)}) collective-permute-start(f32[264,128]{1,0:T(8,128)} %get-tuple-element.25), channel_id=1, source_target_pairs={{0,16},{1,17},{2,18},{3,19},{4,20},{5,21},{6,22},{7,23},{8,24},{9,... | collective-permute-start | bytes 405512 | tf_op jit(solution)/shard_map/ppermute | solution.py:426
  45.0 12.4 %collective-permute-start.9 = (f32[264,128]{1,0:T(8,128)}, f32[264,128]{1,0:T(8,128)}, u32[]{:S(2)}, u32[]{:S(2)}) collective-permute-start(f32[264,128]{1,0:T(8,128)} %get-tuple-element.26), channel_id=1, source_target_pairs={{0,24},{1,25},{2,26},{3,27},{4,28},{5,29},{6,30},{7,31},{8,0},{9,1... | collective-permute-start | bytes 405512 | tf_op jit(solution)/shard_map/ppermute | solution.py:426

commit v4 on v3

--- a/solution.py
+++ b/solution.py
@@ -218,8 +218,8 @@
             for m in range(MXUS):
                 left = first_w[chunk * CHUNK : (chunk + 1) * CHUNK]
                 pltpu.matmul_acc_lhs(accs[m][chunk], left, 0 if chunk == 0 else None)
-            if chunk == 2 or chunk == 6:
-                k = chunk // 6
+            if chunk == 3 or chunk == 7:
+                k = chunk // 7
                 for m in range(MXUS):
                     right = hidden[other, k * depth : (k + 1) * depth, m * half : (m + 1) * half]
                     pltpu.matmul_push_rhs(right, k, m)

time: 59 us -> 59.2 us (level)
  starting transfers between devices: 17.7 us -> 27.2 us
  Pallas kernels: 25.2 us -> 17 us
  waiting for transfers between devices: 15.7 us -> 14.6 us
    ppermute x10, starting transfers between devices: 17.7 us -> 27.2 us  [move(): return lax.ppermute(value, axes, pairs)]
    pallas_call x1, Pallas kernels: 21.2 us -> 13 us  [shards(): pl.pallas_call(functools.partial(head_kernel, (n_cplx, parts, cpx_dev, sl...]
    ppermute x10, waiting for transfers between devices: 15.7 us -> 14.6 us  [move(): return lax.ppermute(value, axes, pairs)]
  transfers between devices with their start and end apart: 10 -> 10, of which waited for: 7 -> 6; matrix products, arithmetic and copies ran while one was open for 0% -> 0% of each run, Pallas kernels for 0% -> 0%
where the time goes in v4:
time: 59.2 us; the launch traced here: 59.5 us
  starting transfers between devices  27.2 us (46%)
  Pallas kernels  17 us (29%)
  waiting for transfers between devices  14.6 us (25%)
  between operations  0.65 us (1%)
    ppermute x10, starting transfers between devices, move(): return lax.ppermute(value, axes, pairs)  27.2 us
    ppermute x10, waiting for transfers between devices, move(): return lax.ppermute(value, axes, pairs)  14.6 us
    pallas_call x1, Pallas kernels, shards(): pl.pallas_call(functools.partial(head_kernel, (n_cplx, parts, cpx_dev, sl...  13 us
    pallas_call x1, Pallas kernels, shards(): pl.pallas_call(functools.partial(place_kernel, (n_cplx, parts, cpx_dev, s...  2.13 us
    pallas_call x1, Pallas kernels, shards(): pl.pallas_call(functools.partial(finish_kernel, (parts, cpx_dev, blocks,...  1.88 us
  transfers between devices with their start and end apart: 10, of which 6 were waited for; matrix products, arithmetic and copies ran while one was open for 0% of the time, Pallas kernels for 0%

profile of v4, /device:TPU:9, one launch (start us, length us, event | category | flops | bytes accessed | tf_op | source)
XLA Modules:
  0.0 59.5 jit_solution(237007951123111406)
XLA Ops:
  0.6 13.0 %shard_map.112 = (f32[72,128]{1,0:T(8,128)}, f32[72,128]{1,0:T(8,128)}, f32[72,128]{1,0:T(8,128)}, f32[72,128]{1,0:T(8,128)}, f32[72,128]{1,0:T(8,128)}, /*index...) custom-call(bf16[3,128,128,128]{3,2,1,0:T(8,128)(2,1)} %refs_0_.1, s32[3,96]{1,0:T(4,128)} %bitcast.5, ...), custom_call_target="tpu_custom_call" | custom-call | tf_op jit(solution)/shard_map/pallas_call | solution.py:429
  13.6 3.5 %collective-permute-start = (f32[72,128]{1,0:T(8,128)}, f32[72,128]{1,0:T(8,128)}, u32[]{:S(2)}, u32[]{:S(2)}) collective-permute-start(f32[72,128]{1,0:T(8,128)} %get-tuple-element.16), channel_id=1, source_target_pairs={{0,4},{1,5},{2,6},{3,7},{4,0},{5,1},{6,2},{7,3},{8,12},{9,13},{10,... | collective-permute-start | bytes 110600 | tf_op jit(solution)/shard_map/ppermute | solution.py:426
  17.1 13.6 %collective-permute-start.1 = (f32[72,128]{1,0:T(8,128)}, f32[72,128]{1,0:T(8,128)}, u32[]{:S(2)}, u32[]{:S(2)}) collective-permute-start(f32[72,128]{1,0:T(8,128)} %get-tuple-element.17), channel_id=1, source_target_pairs={{0,1},{1,2},{2,3},{3,0},{4,5},{5,6},{6,7},{7,4},{8,9},{9,10},{10,1... | collective-permute-start | bytes 110600 | tf_op jit(solution)/shard_map/ppermute | solution.py:426
  30.8 1.4 %collective-permute-start.2 = (f32[72,128]{1,0:T(8,128)}, f32[72,128]{1,0:T(8,128)}, u32[]{:S(2)}, u32[]{:S(2)}) collective-permute-start(f32[72,128]{1,0:T(8,128)} %get-tuple-element.18), channel_id=1, source_target_pairs={{0,5},{1,6},{2,7},{3,4},{4,1},{5,2},{6,3},{7,0},{8,13},{9,14},{10,... | collective-permute-start | bytes 110600 | tf_op jit(solution)/shard_map/ppermute | solution.py:426
  32.2 0.0 collective-permute-start.3
  32.2 1.5 %collective-permute-start.4 = (f32[72,128]{1,0:T(8,128)}, f32[72,128]{1,0:T(8,128)}, u32[]{:S(2)}, u32[]{:S(2)}) collective-permute-start(f32[72,128]{1,0:T(8,128)} %get-tuple-element.20), channel_id=1, source_target_pairs={{0,6},{1,7},{2,4},{3,5},{4,2},{5,3},{6,0},{7,1},{8,14},{9,15},{10,... | collective-permute-start | bytes 110600 | tf_op jit(solution)/shard_map/ppermute | solution.py:426
  33.6 0.0 collective-permute-done.rest_1_
  33.6 0.7 %collective-permute-start.5 = (f32[72,128]{1,0:T(8,128)}, f32[72,128]{1,0:T(8,128)}, u32[]{:S(2)}, u32[]{:S(2)}) collective-permute-start(f32[72,128]{1,0:T(8,128)} %get-tuple-element.21), channel_id=1, source_target_pairs={{0,3},{1,0},{2,1},{3,2},{4,7},{5,4},{6,5},{7,6},{8,11},{9,8},{10,9... | collective-permute-start | bytes 110600 | tf_op jit(solution)/shard_map/ppermute | solution.py:426
  34.4 0.0 collective-permute-done.1.rest_2_
  34.4 1.6 %collective-permute-start.6 = (f32[72,128]{1,0:T(8,128)}, f32[72,128]{1,0:T(8,128)}, u32[]{:S(2)}, u32[]{:S(2)}) collective-permute-start(f32[72,128]{1,0:T(8,128)} %get-tuple-element.22), channel_id=1, source_target_pairs={{0,7},{1,4},{2,5},{3,6},{4,3},{5,0},{6,1},{7,2},{8,15},{9,12},{10,... | collective-permute-start | bytes 110600 | tf_op jit(solution)/shard_map/ppermute | solution.py:426
  36.0 0.0 collective-permute-done.2.rest_3_
  36.0 0.0 collective-permute-done.3.rest_4_
  36.0 0.3 collective-permute-done.4.rest_5_
  36.3 1.3 %collective-permute-done.5.rest_6_ = f32[72,128]{1,0:T(8,128)} collective-permute-done((f32[72,128]{1,0:T(8,128)}, f32[72,128]{1,0:T(8,128)}, u32[]{:S(2)}, u32[]{:S(2)}) %collective-permute-start.5) | collective-permute-done | bytes 36896 | tf_op jit(solution)/shard_map/ppermute | solution.py:426
  37.6 1.3 %collective-permute-done.6.rest_7_ = f32[72,128]{1,0:T(8,128)} collective-permute-done((f32[72,128]{1,0:T(8,128)}, f32[72,128]{1,0:T(8,128)}, u32[]{:S(2)}, u32[]{:S(2)}) %collective-permute-start.6) | collective-permute-done | bytes 36896 | tf_op jit(solution)/shard_map/ppermute | solution.py:426
  39.0 2.1 %shard_map.113 = (f32[264,128]{1,0:T(8,128)}, f32[264,128]{1,0:T(8,128)}, f32[264,128]{1,0:T(8,128)}, f32[264,128]{1,0:T(8,128)}) custom-call(s32[3,96]{1,0:T(4,128)} %bitcast.6, f32[72,128]{1,0:T(8,128)} %get-tuple-element.15.rest_0_, f32[72,128]{1,0:T(8,128)} %collective-permute-done.rest_1_, f32[72,128]{1,0:T(8,128)} %collective-permute-done.1.rest_2_, ...), custom_call_target="tpu_custom_call" | custom-call | tf_op jit(solution)/shard_map/pallas_call | solution.py:483
  41.1 0.0 collective-permute-start.7
  41.1 4.9 %collective-permute-start.8 = (f32[264,128]{1,0:T(8,128)}, f32[264,128]{1,0:T(8,128)}, u32[]{:S(2)}, u32[]{:S(2)}) collective-permute-start(f32[264,128]{1,0:T(8,128)} %get-tuple-element.25), channel_id=1, source_target_pairs={{0,16},{1,17},{2,18},{3,19},{4,20},{5,21},{6,22},{7,23},{8,24},{9,... | collective-permute-start | bytes 405512 | tf_op jit(solution)/shard_map/ppermute | solution.py:426
  46.0 0.0 collective-permute-start.9
  46.0 2.1 %collective-permute-done.7.rest_1_ = f32[264,128]{1,0:T(8,128)} collective-permute-done((f32[264,128]{1,0:T(8,128)}, f32[264,128]{1,0:T(8,128)}, u32[]{:S(2)}, u32[]{:S(2)}) %collective-permute-start.7) | collective-permute-done | bytes 135200 | tf_op jit(solution)/shard_map/ppermute | solution.py:426
  48.0 7.0 %collective-permute-done.8.rest_2_ = f32[264,128]{1,0:T(8,128)} collective-permute-done((f32[264,128]{1,0:T(8,128)}, f32[264,128]{1,0:T(8,128)}, u32[]{:S(2)}, u32[]{:S(2)}) %collective-permute-start.8) | collective-permute-done | bytes 135200 | tf_op jit(solution)/shard_map/ppermute | solution.py:426
  55.1 2.5 %collective-permute-done.9.rest_3_ = f32[264,128]{1,0:T(8,128)} collective-permute-done((f32[264,128]{1,0:T(8,128)}, f32[264,128]{1,0:T(8,128)}, u32[]{:S(2)}, u32[]{:S(2)}) %collective-permute-start.9) | collective-permute-done | bytes 135200 | tf_op jit(solution)/shard_map/ppermute | solution.py:426
  57.6 1.9 %shard_map.114 = (f32[1,64,512]{2,1,0:T(8,128)}, f32[1,64]{1,0:T(1,128)}, f32[1]{0:T(128)}) custom-call(s32[4]{0:T(128)} %lengths_ref.1, s32[4,512]{1,0:T(4,128)} %resolved_ref.1, f32[264,128]{1,0:T(8,128)} %get-tuple-element.23.rest_0_, f32[264,128]{1,0:T(8,128)} %collective-permute-done.7.rest_1_, f32[264,128]{1,0:T(8,128)} %collective-permute-done.8.rest_2_, ...), custom_call_target="tpu_custom_call" | custom-call | tf_op jit(solution)/shard_map/pallas_call | solution.py:495
Async XLA Ops:
  13.6 20.0 %collective-permute-start = (f32[72,128]{1,0:T(8,128)}, f32[72,128]{1,0:T(8,128)}, u32[]{:S(2)}, u32[]{:S(2)}) collective-permute-start(f32[72,128]{1,0:T(8,128)} %get-tuple-element.16), channel_id=1, source_target_pairs={{0,4},{1,5},{2,6},{3,7},{4,0},{5,1},{6,2},{7,3},{8,12},{9,13},{10,... | collective-permute-start | bytes 110600 | tf_op jit(solution)/shard_map/ppermute | solution.py:426
  17.1 17.2 %collective-permute-start.1 = (f32[72,128]{1,0:T(8,128)}, f32[72,128]{1,0:T(8,128)}, u32[]{:S(2)}, u32[]{:S(2)}) collective-permute-start(f32[72,128]{1,0:T(8,128)} %get-tuple-element.17), channel_id=1, source_target_pairs={{0,1},{1,2},{2,3},{3,0},{4,5},{5,6},{6,7},{7,4},{8,9},{9,10},{10,1... | collective-permute-start | bytes 110600 | tf_op jit(solution)/shard_map/ppermute | solution.py:426
  30.8 5.2 %collective-permute-start.2 = (f32[72,128]{1,0:T(8,128)}, f32[72,128]{1,0:T(8,128)}, u32[]{:S(2)}, u32[]{:S(2)}) collective-permute-start(f32[72,128]{1,0:T(8,128)} %get-tuple-element.18), channel_id=1, source_target_pairs={{0,5},{1,6},{2,7},{3,4},{4,1},{5,2},{6,3},{7,0},{8,13},{9,14},{10,... | collective-permute-start | bytes 110600 | tf_op jit(solution)/shard_map/ppermute | solution.py:426
  32.2 3.8 %collective-permute-start.3 = (f32[72,128]{1,0:T(8,128)}, f32[72,128]{1,0:T(8,128)}, u32[]{:S(2)}, u32[]{:S(2)}) collective-permute-start(f32[72,128]{1,0:T(8,128)} %get-tuple-element.19), channel_id=1, source_target_pairs={{0,2},{1,3},{2,0},{3,1},{4,6},{5,7},{6,4},{7,5},{8,10},{9,11},{10,... | collective-permute-start | bytes 110600 | tf_op jit(solution)/shard_map/ppermute | solution.py:426
  32.2 4.2 %collective-permute-start.4 = (f32[72,128]{1,0:T(8,128)}, f32[72,128]{1,0:T(8,128)}, u32[]{:S(2)}, u32[]{:S(2)}) collective-permute-start(f32[72,128]{1,0:T(8,128)} %get-tuple-element.20), channel_id=1, source_target_pairs={{0,6},{1,7},{2,4},{3,5},{4,2},{5,3},{6,0},{7,1},{8,14},{9,15},{10,... | collective-permute-start | bytes 110600 | tf_op jit(solution)/shard_map/ppermute | solution.py:426
  33.6 4.0 %collective-permute-start.5 = (f32[72,128]{1,0:T(8,128)}, f32[72,128]{1,0:T(8,128)}, u32[]{:S(2)}, u32[]{:S(2)}) collective-permute-start(f32[72,128]{1,0:T(8,128)} %get-tuple-element.21), channel_id=1, source_target_pairs={{0,3},{1,0},{2,1},{3,2},{4,7},{5,4},{6,5},{7,6},{8,11},{9,8},{10,9... | collective-permute-start | bytes 110600 | tf_op jit(solution)/shard_map/ppermute | solution.py:426
  34.4 4.6 %collective-permute-start.6 = (f32[72,128]{1,0:T(8,128)}, f32[72,128]{1,0:T(8,128)}, u32[]{:S(2)}, u32[]{:S(2)}) collective-permute-start(f32[72,128]{1,0:T(8,128)} %get-tuple-element.22), channel_id=1, source_target_pairs={{0,7},{1,4},{2,5},{3,6},{4,3},{5,0},{6,1},{7,2},{8,15},{9,12},{10,... | collective-permute-start | bytes 110600 | tf_op jit(solution)/shard_map/ppermute | solution.py:426
  41.1 7.0 %collective-permute-start.7 = (f32[264,128]{1,0:T(8,128)}, f32[264,128]{1,0:T(8,128)}, u32[]{:S(2)}, u32[]{:S(2)}) collective-permute-start(f32[264,128]{1,0:T(8,128)} %get-tuple-element.24), channel_id=1, source_target_pairs={{0,8},{1,9},{2,10},{3,11},{4,12},{5,13},{6,14},{7,15},{8,16},{9,17... | collective-permute-start | bytes 405512 | tf_op jit(solution)/shard_map/ppermute | solution.py:426
  41.1 14.0 %collective-permute-start.8 = (f32[264,128]{1,0:T(8,128)}, f32[264,128]{1,0:T(8,128)}, u32[]{:S(2)}, u32[]{:S(2)}) collective-permute-start(f32[264,128]{1,0:T(8,128)} %get-tuple-element.25), channel_id=1, source_target_pairs={{0,16},{1,17},{2,18},{3,19},{4,20},{5,21},{6,22},{7,23},{8,24},{9,... | collective-permute-start | bytes 405512 | tf_op jit(solution)/shard_map/ppermute | solution.py:426
  46.0 11.7 %collective-permute-start.9 = (f32[264,128]{1,0:T(8,128)}, f32[264,128]{1,0:T(8,128)}, u32[]{:S(2)}, u32[]{:S(2)}) collective-permute-start(f32[264,128]{1,0:T(8,128)} %get-tuple-element.26), channel_id=1, source_target_pairs={{0,24},{1,25},{2,26},{3,27},{4,28},{5,29},{6,30},{7,31},{8,0},{9,1... | collective-permute-start | bytes 405512 | tf_op jit(solution)/shard_map/ppermute | solution.py:426
